TPU v7x, 1024 devices: a whole 4x8x16 slice. The times are simulated.
1024 devices in a mesh: dp: 8 (over y_lo, core), frame: 8 (over x, y_hi), lon: 16 (over z).
Axes of the slice: x: 4, y: 8 (y_hi: 2, y_lo: 4; y = y_hi * 4 + y_lo), z: 16, core: 2. Of those that a mesh axis runs over, the one named last changes fastest.
Arguments:
- fields: bfloat16 [8, 8, 4, 1440, 1024], P('dp', 'frame', None, 'lon'), may hold values from -6 to 6
- band_rows: int32 [8, 4], P('dp'), may hold values from 0 to 719
- earliest_past_snapshot: int32 [8], P('dp'), may hold values from 0 to 7
- lat_table: bfloat16 [720, 1024], replicated, may hold values from -3 to 3
- norm_gain: float32 [1024], replicated, may hold values from 0.5 to 1.5
- w_in1: bfloat16 [2, 16, 64, 64], P(None, 'lon'), may hold values from -0.5 to 0.5
- b_in1: float32 [2, 1024], P(None, 'lon'), may hold values from -1.5 to 1.5
- w_out2: bfloat16 [2, 16, 64, 64], P(None, 'lon'), may hold values from -0.5 to 0.5
- b_out2: float32 [2, 1024], P(None, 'lon'), may hold values from -0.25 to 0.25
- w_query: bfloat16 [1024, 1024], replicated, may hold values from -0.1875 to 0.1875
- w_keyval: bfloat16 [1024, 512], replicated, may hold values from -0.1875 to 0.1875
- w_output: bfloat16 [1024, 1024], replicated, may hold values from -0.1875 to 0.1875
- score_scale: float32 [16], replicated, may hold values from 0.5 to 100
- spec_cot: bfloat16 [8, 8, 4, 2, 368, 1024], P('dp', 'frame', None, None, None, 'lon'), may hold values from -0.01953125 to 0.01953125
Outputs:
- predicted_output_fields: bfloat16 [8, 8, 4, 1440, 1024], P('dp', 'frame', None, 'lon')
- mask_coefficient2_derivative: float32 [2, 16, 64, 64], P(None, 'lon')
- mask_offset2_derivative: float32 [2, 1024], P(None, 'lon')
All inputs are finite; a program needn't handle non-finite values.
Results may differ from a plain program's by a relative error of at most 0.03.
Values may be sent and summed in bfloat16 or wider, within the bound.
A program may use at most 64 MiB of HBM per device.

v0:
```python
import math

import jax
import jax.numpy as jnp
from jax import lax
from jax.sharding import PartitionSpec as P


def transform_table(length, modes):
    longitude = jnp.arange(length, dtype=jnp.int32)
    zonal_wavenumber = jnp.arange(modes, dtype=jnp.int32)
    turns_mod = longitude[:, None] * zonal_wavenumber[None, :] % length
    angles = turns_mod.astype(jnp.float32) * (2.0 * math.pi / length)
    return jnp.concatenate([jnp.cos(angles), -jnp.sin(angles)], axis=1).astype(jnp.bfloat16)


def inverse_table(forward, modes):
    zonal_wavenumber = jnp.arange(modes, dtype=jnp.int32)
    factor = jnp.where(zonal_wavenumber == 0, 1.0, 2.0).astype(jnp.float32)
    factor = jnp.concatenate([factor, factor])
    return (forward.astype(jnp.float32) * factor[None, :]).astype(jnp.bfloat16)


def block_mix(left, weight):
    return jnp.einsum("rmgc,gce->rmge", left, weight, preferred_element_type=jnp.float32)


def filter_modes(spectrum, w_in1, b_in1, w_out2, b_out2):
    spectral_real = spectrum[:, 0]
    spec_im = spectrum[:, 1]
    first_re = jax.nn.relu(
        block_mix(spectral_real, w_in1[0]) - block_mix(spec_im, w_in1[1]) + b_in1[0]
    ).astype(jnp.bfloat16)
    first_im = jax.nn.relu(
        block_mix(spectral_real, w_in1[1]) + block_mix(spec_im, w_in1[0]) + b_in1[1]
    ).astype(jnp.bfloat16)
    second_re = (
        block_mix(first_re, w_out2[0]) - block_mix(first_im, w_out2[1]) + b_out2[0]
    ).astype(jnp.bfloat16)
    second_im = (
        block_mix(first_re, w_out2[1]) + block_mix(first_im, w_out2[0]) + b_out2[1]
    ).astype(jnp.bfloat16)
    return (first_re, first_im, jnp.concatenate([second_re, second_im], axis=1))


def head_norm(values_in):
    return values_in * lax.rsqrt(jnp.mean(values_in * values_in, axis=-1, keepdims=True) + 1e-06)


def attend(
    queries, keys_all, value_rows_full, query_frame, first_seen, score_scale, kv_heads, head_size
):
    site_count, query_frames, width = queries.shape
    key_frames = keys_all.shape[1]
    groups = width // head_size // kv_heads
    q_five = queries.reshape(site_count, query_frames, kv_heads, groups, head_size)
    k_four = keys_all.reshape(site_count, key_frames, kv_heads, head_size)
    v_four = value_rows_full.reshape(site_count, key_frames, kv_heads, head_size)
    scores = jnp.einsum("sqkgd,stkd->kgqts", q_five, k_four, preferred_element_type=jnp.float32)
    scores = scores * (score_scale.reshape(kv_heads, groups, 1, 1, 1) / math.sqrt(head_size))
    key_ids = jnp.arange(key_frames, dtype=jnp.int32)[None, :, None]
    query_ids = query_frame[:, None, None]
    seen = (key_ids <= query_ids) & (
        (key_ids >= first_seen[None, None, :]) | (key_ids == query_ids)
    )
    scores = jnp.where(seen[None, None], scores, -1e30)
    top_score = jnp.max(scores, axis=-2, keepdims=True)
    weights = jnp.exp(scores - top_score)
    probs = (weights / jnp.sum(weights, axis=-2, keepdims=True)).astype(jnp.bfloat16)
    attended = jnp.einsum("kgqts,stkd->sqkgd", probs, v_four, preferred_element_type=jnp.float32)
    return attended.astype(jnp.bfloat16).reshape(site_count, query_frames, width)


def body(
    fields,
    band_rows,
    earliest_past_snapshot,
    lat_table,
    norm_gain,
    w_in1,
    b_in1,
    w_out2,
    b_out2,
    w_query,
    w_keyval,
    w_output,
    score_scale,
    spec_cot,
):
    samples, _, lat_rows, lon_local, width = fields.shape
    grid_rows = samples * lat_rows
    length = lon_local * lax.axis_size("lon")
    modes = spec_cot.shape[4]
    local_width = spec_cot.shape[5]
    blocks = w_in1.shape[1]
    block_size = w_in1.shape[2]
    forward = transform_table(length, modes)
    backward = inverse_table(forward, modes)
    scale_t = 1.0 / math.sqrt(length)
    lat_count = lat_table.shape[0]
    onehot = (
        band_rows[:, :, None] == jnp.arange(lat_count, dtype=jnp.int32)[None, None, :]
    ).astype(jnp.bfloat16)
    embedding = jnp.dot(
        onehot.reshape(grid_rows, lat_count), lat_table, preferred_element_type=jnp.float32
    )
    inputs = fields[:, 0].astype(jnp.float32) + embedding.reshape(samples, lat_rows, 1, width)
    center = jnp.mean(inputs, axis=-1, keepdims=True)
    spread = jnp.mean(jnp.square(inputs - center), axis=-1, keepdims=True)
    normed = ((inputs - center) * lax.rsqrt(spread + 1e-05) * norm_gain).astype(jnp.bfloat16)
    gathered = lax.all_to_all(
        normed.reshape(grid_rows, lon_local, width), "lon", split_axis=2, concat_axis=1, tiled=True
    )
    spectrum = (
        jnp.einsum("rnc,nk->rkc", gathered, forward, preferred_element_type=jnp.float32) * scale_t
    ).astype(jnp.bfloat16)
    spectrum = spectrum.reshape(grid_rows, 2, modes, blocks, block_size)
    first_re, first_im, mixed = filter_modes(
        spectrum,
        w_in1,
        b_in1.reshape(2, blocks, block_size),
        w_out2,
        b_out2.reshape(2, blocks, block_size),
    )
    mixed = mixed.reshape(grid_rows, 2 * modes, local_width)
    grid_part = (
        jnp.einsum("rkc,nk->rnc", mixed, backward, preferred_element_type=jnp.float32) * scale_t
    ).astype(jnp.bfloat16)
    returned = lax.all_to_all(grid_part, "lon", split_axis=1, concat_axis=2, tiled=True)
    hidden = (
        inputs + returned.reshape(samples, lat_rows, lon_local, width).astype(jnp.float32)
    ).astype(jnp.bfloat16)
    cotangent = spec_cot.reshape(grid_rows, 2, modes, blocks, block_size)
    grad_re = jnp.einsum(
        "rmgc,rmge->gce", first_re, cotangent[:, 0], preferred_element_type=jnp.float32
    )
    grad_re = grad_re + jnp.einsum(
        "rmgc,rmge->gce", first_im, cotangent[:, 1], preferred_element_type=jnp.float32
    )
    grad_im = jnp.einsum(
        "rmgc,rmge->gce", first_re, cotangent[:, 1], preferred_element_type=jnp.float32
    )
    grad_im = grad_im - jnp.einsum(
        "rmgc,rmge->gce", first_im, cotangent[:, 0], preferred_element_type=jnp.float32
    )
    bias_terms = jnp.sum(cotangent.astype(jnp.float32), axis=(0, 2)).reshape(2, local_width)
    mask_coefficient2_derivative, mask_offset2_derivative = lax.psum(
        (jnp.stack([grad_re, grad_im]), bias_terms), ("dp", "frame")
    )
    site_count = grid_rows * lon_local
    tokens = hidden.reshape(site_count, width)
    head_count = score_scale.shape[0]
    head_size = width // head_count
    kv_width = w_keyval.shape[1] // 2
    kv_heads = kv_width // head_size
    query = jnp.dot(tokens, w_query, preferred_element_type=jnp.float32).reshape(
        site_count, head_count, head_size
    )
    qnorm = head_norm(query).astype(jnp.bfloat16).reshape(site_count, 1, width)
    keyval = jnp.dot(tokens, w_keyval, preferred_element_type=jnp.float32)
    knorm = (
        head_norm(keyval[:, :kv_width].reshape(site_count, kv_heads, head_size))
        .astype(jnp.bfloat16)
        .reshape(site_count, 1, kv_width)
    )
    values = keyval[:, kv_width:].astype(jnp.bfloat16).reshape(site_count, 1, kv_width)
    first_seen = jnp.broadcast_to(
        earliest_past_snapshot[:, None], (samples, lat_rows * lon_local)
    ).reshape(site_count)
    own_frame = lax.axis_index("frame")
    keys_all, value_rows_full = (
        lax.all_gather(knorm, "frame", axis=1, tiled=True),
        lax.all_gather(values, "frame", axis=1, tiled=True),
    )
    query_frame = jnp.reshape(own_frame, (1,))
    attended = attend(
        qnorm, keys_all, value_rows_full, query_frame, first_seen, score_scale, kv_heads, head_size
    )
    output = jnp.dot(
        attended.reshape(site_count, width), w_output, preferred_element_type=jnp.float32
    )
    predicted_output_fields = (
        (tokens.astype(jnp.float32) + output)
        .astype(jnp.bfloat16)
        .reshape(samples, 1, lat_rows, lon_local, width)
    )
    return (predicted_output_fields, mask_coefficient2_derivative, mask_offset2_derivative)


def solution(mesh):
    placed = (
        P("dp", "frame", None, "lon", None),
        P("dp", None),
        P("dp"),
        P(),
        P(),
        P(None, "lon", None, None),
        P(None, "lon"),
        P(None, "lon", None, None),
        P(None, "lon"),
        P(),
        P(),
        P(),
        P(),
        P("dp", "frame", None, None, None, "lon"),
    )
    return jax.shard_map(
        body,
        mesh=mesh,
        in_specs=placed,
        out_specs=(P("dp", "frame", None, "lon", None), P(None, "lon", None, None), P(None, "lon")),
        check_vma=False,
    )
```

profile of v0, /device:TPU:1, one launch (start us, length us, event | category | flops | bytes accessed | tf_op | source)
XLA Modules:
  0.0 598.7 jit_solution(8412278590125999928)
XLA Ops:
  7.2 2.0 copy.90
  15.0 19.5 %all-to-all-start = ((bf16[4,90,1024]{1,0,2:T(4,128)(2,1)}), bf16[4,90,1024]{1,0,2:T(4,128)(2,1)}, u32[]{:S(2)}, u32[]{:S(2)}) async-start(bf16[4,90,1024]{1,0,2:T(4,128)(2,1)} %copy.93), calls=%async_computation | async-start | bytes 2097152 | tf_op jit(solution)/shard_map/all_to_all | solution.py:111
  36.4 10.4 %negate_convert_fusion = (bf16[1440,368]{1,0:T(8,128)(2,1)}, bf16[1440,368]{1,0:T(8,128)(2,1)}) fusion(), kind=kLoop, calls=%fused_computation.13 | loop fusion | flops 6359040 | bytes 2119680 | tf_op jit(solution)/shard_map/convert.11
  46.8 32.6 %all-to-all-done = bf16[4,90,1024]{1,0,2:T(4,128)(2,1)} async-done(((bf16[4,90,1024]{1,0,2:T(4,128)(2,1)}), bf16[4,90,1024]{1,0,2:T(4,128)(2,1)}, u32[]{:S(2)}, u32[]{:S(2)}) %all-to-all-start) | async-done | bytes 737312 | tf_op jit(solution)/shard_map/all_to_all | solution.py:111
  82.4 2.9 all_to_all.23
  85.4 2.7 fusion.15
  95.9 3.4 copy.102
  99.3 2.8 reshape.446
  102.1 13.2 %all-to-all-start.1 = ((bf16[16,2,11520]{2,1,0:T(2,128)(2,1)}), bf16[16,2,11520]{2,1,0:T(2,128)(2,1)}, u32[]{:S(2)}, u32[]{:S(2)}) async-start(bf16[16,2,11520]{2,1,0:T(2,128)(2,1)} %reshape.446), calls=%async_computation.1 | async-start | bytes 1474560 | tf_op jit(solution)/shard_map/all_to_all | solution.py:129
  117.1 2.7 reshape.420
  121.2 2.8 add.171
  124.0 23.5 %all-to-all-done.1 = bf16[16,2,11520]{2,1,0:T(2,128)(2,1)} async-done(((bf16[16,2,11520]{2,1,0:T(2,128)(2,1)}), bf16[16,2,11520]{2,1,0:T(2,128)(2,1)}, u32[]{:S(2)}, u32[]{:S(2)}) %all-to-all-start.1) | async-done | bytes 737312 | tf_op jit(solution)/shard_map/all_to_all | solution.py:129
  147.5 2.9 reshape.447
  150.4 3.2 copy.144
  153.6 3.4 reshape.444
  157.0 2.7 add_convert_fusion.1
  162.8 1.9 copy.108
  172.1 3.9 copy.112
  184.9 352.4 %all-reduce = (f32[2,1,64,64]{3,2,1,0:T(8,128)}, f32[2,64]{1,0:T(2,128)}) all-reduce(f32[2,1,64,64]{3,2,1,0:T(8,128)S(1)} %pad_maximum_fusion.4, f32[2,64]{1,0:T(2,128)} %convert_reduce_fusion), channel_id=1, replica_groups=mesh['dp'=8,'frame'=8,'lon'=16] {'dp','frame'}, use_global_device_ids=true, to_apply=%region_6.7 | all-reduce | flops 8320 | bytes 66560 | tf_op jit(solution)/shard_map/psum | solution.py:147
  537.2 3.8 copy.103
  541.0 2.8 fusion.8
  546.4 3.1 multiply_reduce_fusion.1
  549.7 2.2 copy.114
  551.9 2.6 copy.110
  554.5 4.3 copy.113
  558.8 2.6 copy.106
  561.4 6.0 %copy.115 = bf16[360,8,4,64]{3,1,2,0:T(8,128)(2,1)} copy(bf16[360,8,4,64]{0,3,2,1:T(8,128)(2,1)} %bitcast.242) | data formatting | bytes 2949120 | tf_op jit(solution)/shard_map/reshape | solution.py:58
  567.4 4.9 fusion.68
  572.4 3.6 fusion
  576.0 6.3 %fusion.12 = bf16[360,1,4,4,64]{4,3,2,0,1:T(4,128)(2,1)} fusion(bf16[360,8,4,64]{3,1,2,0:T(8,128)(2,1)S(1)} %copy-done.4, f32[4,4,360]{1,2,0:T(8,128)S(1)} %fusion, f32[4,4,1,8,360]{3,1,4,0,2:T(4,128)S(1)} %get-tuple-element.26, f32[4,4,360]{1,2,0:T(8,128)S(1)} %get-tuple-element.25), kind=kOutput, calls=%fused_computation.34 | convolution fusion | flops 6405120 | bytes 2442240 | tf_op jit(solution)/shard_map/kgqts,stkd->sqkgd/dot_general | solution.py:70
  582.4 3.8 copy.117
  586.2 3.0 add_convert_fusion
  (101 shorter events, 45.5 us)
Async XLA Ops:
  7.2 579.0 %copy-start = (bf16[1024,1024]{1,0:T(8,128)(2,1)S(1)}, bf16[1024,1024]{1,0:T(8,128)(2,1)}, u32[]{:S(2)}) copy-start(bf16[1024,1024]{1,0:T(8,128)(2,1)} %param.25) | copy-start | bytes 6291460
  9.1 3.2 copy-start.11
  13.2 22.0 %copy-start.18 = (f32[2,64]{1,0:T(2,128)S(1)}, f32[2,64]{1,0:T(2,128)}, u32[]{:S(2)}) copy-start(f32[2,64]{1,0:T(2,128)} %param.20) | copy-start | bytes 1540
  13.2 22.6 %copy-start.19 = (f32[2,64]{1,0:T(2,128)S(1)}, f32[2,64]{1,0:T(2,128)}, u32[]{:S(2)}) copy-start(f32[2,64]{1,0:T(2,128)} %param.22) | copy-start | bytes 1540
  15.0 64.4 %all-to-all-start = ((bf16[4,90,1024]{1,0,2:T(4,128)(2,1)}), bf16[4,90,1024]{1,0,2:T(4,128)(2,1)}, u32[]{:S(2)}, u32[]{:S(2)}) async-start(bf16[4,90,1024]{1,0,2:T(4,128)(2,1)} %copy.93), calls=%async_computation | async-start | bytes 2097152 | tf_op jit(solution)/shard_map/all_to_all | solution.py:111
  90.2 1.6 copy-start.8
  90.3 1.8 copy-start.17
  90.3 2.0 copy-start.9
  90.3 2.5 copy-start.16
  90.8 2.2 copy-start.15
  91.8 1.5 copy-start.14
  92.3 1.4 copy-start.5
  92.3 1.6 copy-start.6
  92.3 1.6 copy-start.12
  102.1 45.4 %all-to-all-start.1 = ((bf16[16,2,11520]{2,1,0:T(2,128)(2,1)}), bf16[16,2,11520]{2,1,0:T(2,128)(2,1)}, u32[]{:S(2)}, u32[]{:S(2)}) async-start(bf16[16,2,11520]{2,1,0:T(2,128)(2,1)} %reshape.446), calls=%async_computation.1 | async-start | bytes 1474560 | tf_op jit(solution)/shard_map/all_to_all | solution.py:129
  115.4 436.6 %all-gather.7.cloned.1.call-start = ((), (), s32[]{:S(2)}) async-start(), calls=%async_computation.3 | async-start | bytes 1658880 | tf_op jit(solution)/shard_map/all_gather | solution.py:172
  157.0 3.6 copy-start.7
  159.8 0.9 copy-start.1
  161.2 0.9 copy-start.3
  170.3 388.5 %all-gather.5.cloned.1.call-start = ((), (), s32[]{:S(2)}) async-start(), calls=%async_computation.2 | async-start | bytes 1658880 | tf_op jit(solution)/shard_map/all_gather | solution.py:173
  561.4 6.0 %copy-start.10 = (pred[8,360]{0,1:T(8,128)(4,1)S(1)}, pred[8,360]{0,1:T(8,128)(4,1)}, u32[]{:S(2)}) copy-start(pred[8,360]{0,1:T(8,128)(4,1)} %copy.107) | copy-start | bytes 8644
  561.4 6.0 %copy-start.13 = (f32[4,4]{1,0:T(4,128)S(1)}, f32[4,4]{1,0:T(4,128)}, u32[]{:S(2)}) copy-start(f32[4,4]{1,0:T(4,128)} %div.38) | copy-start | bytes 196
  572.4 3.6 copy-start.4
  582.4 3.8 copy-start.2
Sparse Core Ops, SparseCore 0:
  170.4 84.0 all-gather.6
  258.8 77.3 all-gather.4
where the time goes:
time: 600 us; the launch traced here: 599 us
  blocking collectives  352 us (59%)
  local copies, waits for them, and re-layouts  83.6 us (14%)
  waiting for transfers between devices  56.2 us (9%)
  starting transfers between devices  33 us (6%)
  other arithmetic  31.8 us (5%)
  matrix products  26.6 us (4%)
  between operations  15.2 us (3%)
    psum x1, blocking collectives, body(): lax.psum((jnp.stack([grad_re, grad_im]), bias_terms), ('dp', 'frame'))  352 us
    all_to_all x1, waiting for transfers between devices, body(): lax.all_to_all(normed.reshape(grid_rows, lon_local, width), 'lon', split_...  32.6 us
    all_to_all x1, waiting for transfers between devices, body(): lax.all_to_all(grid_part, 'lon', split_axis=1, concat_axis=2, tiled=True)  23.5 us
    all_to_all x1, starting transfers between devices, body(): lax.all_to_all(normed.reshape(grid_rows, lon_local, width), 'lon', split_...  19.5 us
    unnamed x46, local copies, waits for them, and re-layouts  16.1 us
    all_to_all x1, starting transfers between devices, body(): lax.all_to_all(grid_part, 'lon', split_axis=1, concat_axis=2, tiled=True)  13.2 us
  transfers between devices with their start and end apart: 4, of which 2 were waited for; matrix products, arithmetic and copies ran while one was open for 9% of the time, Pallas kernels for 0%

commit v1 on v0

v1 whole, which is shorter than its diff:
```python
import functools
import math

import jax
import jax.numpy as jnp
import numpy as np
from jax import lax
from jax.experimental import pallas as pl
from jax.experimental.pallas import tpu as pltpu
from jax.sharding import PartitionSpec as P

MESH = pl.DeviceIdType.MESH
F32 = jnp.float32
BF16 = jnp.bfloat16


def lanes_below(shape, bound):
    return lax.broadcasted_iota(jnp.int32, shape, len(shape) - 1) < bound


def split_two(value):
    high = value.astype(BF16)
    return high, (value - high.astype(F32)).astype(BF16)


def dot32(left, right, dims=(((1,), (0,)), ((), ()))):
    return lax.dot_general(left, right, dims, preferred_element_type=F32)


def angle_tables(length, local, parts, padded, modes, wide):
    near = np.zeros((2, padded, wide), np.float64)
    far = np.zeros((2, parts, 1, wide), np.float64)
    wave = np.arange(modes)
    turn = 2.0 * np.pi / length
    inner = (np.arange(local)[:, None] * wave[None, :]) % length
    near[0, :local, :modes] = np.cos(turn * inner)
    near[1, :local, :modes] = np.sin(turn * inner)
    outer = (np.arange(parts)[:, None] * local * wave[None, :]) % length
    far[0, :, 0, :modes] = np.cos(turn * outer)
    far[1, :, 0, :modes] = np.sin(turn * outer)
    return near.astype(np.float32), far.astype(np.float32)


def layer_kernel(
    geo,
    first_ref,
    fields_ref,
    embed_ref,
    gain_ref,
    w1_ref,
    b1_ref,
    w2_ref,
    b2_ref,
    near_ref,
    far_ref,
    scale_ref,
    cot_ref,
    wq_hbm,
    wkv_hbm,
    wo_hbm,
    out_ref,
    grad_ref,
    wq,
    wkv,
    wo,
    table,
    mix1,
    mix2,
    brow,
    send1,
    recv1,
    send2,
    recv2,
    sendh,
    recvh,
    sendo,
    recvo,
    qs,
    kx,
    vx,
    scores,
    top,
    total,
    attended,
    acc,
    sums_send,
    sums_recv,
    weight_sem,
    own_sem,
    z_send,
    z_recv,
    f_send,
    f_recv,
    s_send,
    s_recv,
):
    n, nf, nd = geo["lon"], geo["frame"], geo["dp"]
    local, padded, modes, wide = geo["local"], geo["padded"], geo["modes"], geo["wide"]
    width, slab = geo["width"], geo["slab"]
    heads, kv_heads, hd = geo["heads"], geo["kv_heads"], geo["hd"]
    kv_width = kv_heads * hd
    scale_t = 1.0 / math.sqrt(local * n)
    me = lax.axis_index("lon")
    my_frame = lax.axis_index("frame")
    my_dp = lax.axis_index("dp")

    def partner(index, bit):
        return index + bit * (1 - 2 * ((index // bit) % 2))

    sum_steps = []
    bit = 1
    while bit < nd:
        sum_steps.append(("dp", partner(my_dp, bit)))
        bit *= 2
    bit = 1
    while bit < nf:
        sum_steps.append(("frame", partner(my_frame, bit)))
        bit *= 2
    dp_partners = [who for axis, who in sum_steps if axis == "dp"]

    barrier = pltpu.get_barrier_semaphore()

    @pl.loop(1, n)
    def _(o):
        pl.semaphore_signal(
            barrier, inc=1, device_id={"lon": lax.rem(me + o, n)}, device_id_type=MESH
        )

    @pl.loop(1, nf)
    def _(o):
        pl.semaphore_signal(
            barrier, inc=1, device_id={"frame": lax.rem(my_frame + o, nf)}, device_id_type=MESH
        )

    for who in dp_partners:
        pl.semaphore_signal(barrier, inc=1, device_id={"dp": who}, device_id_type=MESH)

    weight_copies = [
        pltpu.make_async_copy(src, dst, weight_sem.at[i])
        for i, (src, dst) in enumerate(((wq_hbm, wq), (wkv_hbm, wkv), (wo_hbm, wo)))
    ]
    for copy in weight_copies:
        copy.start()

    send1[...] = jnp.zeros_like(send1)
    sendh[...] = jnp.zeros_like(sendh)

    def z_copy(src, dst, stage, p, o, target, slot):
        return pltpu.make_async_remote_copy(
            src_ref=src.at[p, target],
            dst_ref=dst.at[p, slot],
            send_sem=z_send.at[stage, p, o],
            recv_sem=z_recv.at[stage, p, o],
            device_id={"lon": target},
            device_id_type=MESH,
        )

    def f_copy(src, dst, stage, p, o, target, slot):
        return pltpu.make_async_remote_copy(
            src_ref=src.at[p, target],
            dst_ref=dst.at[p, slot],
            send_sem=f_send.at[stage, p, o],
            recv_sem=f_recv.at[stage, p, o],
            device_id={"frame": target},
            device_id_type=MESH,
        )

    def start_all(maker, src, dst, stage, p, size, mine, own):
        @pl.loop(1, size)
        def _(o):
            maker(src, dst, stage, p, o, lax.rem(mine + o, size), mine).start()

        pltpu.make_async_copy(src.at[p, mine], dst.at[p, mine], own_sem.at[own, p]).start()

    def wait_recvs(maker, src, dst, stage, p, size, mine, own):
        pltpu.make_async_copy(src.at[p, mine], dst.at[p, mine], own_sem.at[own, p]).wait()

        @pl.loop(1, size)
        def _(o):
            peer = lax.rem(mine + size - o, size)
            maker(src, dst, stage, p, o, peer, peer).wait_recv()

    def wait_sends(maker, src, dst, stage, p, size, mine):
        @pl.loop(1, size)
        def _(o):
            maker(src, dst, stage, p, o, lax.rem(mine + o, size), mine).wait_send()

    half = lanes_below((local, 128), 64)

    def normalize(p, r):
        cells = fields_ref[2 * p + r].astype(F32) + embed_ref[2 * p + r]
        cells = cells - jnp.mean(cells, axis=-1, keepdims=True)
        spread = jnp.mean(cells * cells, axis=-1, keepdims=True)
        return cells * lax.rsqrt(spread + 1e-05) * gain_ref[...]

    @pl.loop(0, 2)
    def _(p):
        row_a = normalize(p, 0)
        row_b = normalize(p, 1)
        for s in range(n // 2):
            part_a = row_a[:, s * 128 : (s + 1) * 128]
            part_b = row_b[:, s * 128 : (s + 1) * 128]
            even = jnp.where(half, part_a, pltpu.roll(part_b, 64, 1))
            odd = jnp.where(half, pltpu.roll(part_a, 64, 1), part_b)
            send1[p, 2 * s, 0:local, :] = even.astype(BF16)
            send1[p, 2 * s + 1, 0:local, :] = odd.astype(BF16)

        @pl.when(p == 0)
        def _():
            pl.semaphore_wait(barrier, (n - 1) + (nf - 1) + len(dp_partners))

        start_all(z_copy, send1, recv1, 0, p, n, me, 0)

    near_cos, near_sin = near_ref[0], near_ref[1]

    @pl.loop(0, n)
    def _(s):
        far_cos, far_sin = far_ref[0, s], far_ref[1, s]
        rows = pl.ds(pl.multiple_of(s * padded, padded), padded)
        table[rows, 0:wide] = (near_cos * far_cos - near_sin * far_sin).astype(BF16)
        table[rows, wide : 2 * wide] = (-(near_sin * far_cos + near_cos * far_sin)).astype(BF16)

    columns = []
    for w_ref, mix, b_ref in ((w1_ref, mix1, b1_ref), (w2_ref, mix2, b2_ref)):
        brow[0:64, 0:64] = w_ref[0].astype(F32)
        brow[0:64, 64:128] = w_ref[1].astype(F32)
        brow[64:128, 0:64] = -w_ref[1].astype(F32)
        brow[64:128, 64:128] = w_ref[0].astype(F32)
        mix[...] = brow[...].T.astype(BF16)
        brow[0:1, 0:64] = b_ref[0:1, :]
        brow[0:1, 64:128] = b_ref[1:2, :]
        columns.append(jnp.broadcast_to(brow[0:1, :], (128, 128)).T[:, 0:1])
    column1, column2 = columns
    wave = lax.broadcasted_iota(jnp.int32, (128, wide), 1)
    factor = jnp.where(wave == 0, 1.0, 2.0)

    acc[...] = jnp.zeros_like(acc)

    @pl.loop(0, 2)
    def _(p):
        wait_recvs(z_copy, send1, recv1, 0, p, n, me, 0)
        gathered = recv1[p].reshape(n * padded, 128)
        spectrum = dot32(gathered.T, table[...]) * scale_t
        cos_part = spectrum[:, 0:wide].astype(BF16)
        sin_part = spectrum[:, wide : 2 * wide].astype(BF16)
        mixed_re, mixed_im = [], []
        for r in range(2):
            stacked = jnp.concatenate(
                [cos_part[64 * r : 64 * r + 64], sin_part[64 * r : 64 * r + 64]], axis=0
            )
            first = jnp.maximum(dot32(mix1[...], stacked) + column1, 0.0).astype(BF16)
            second = (dot32(mix2[...], first) + column2).astype(BF16)
            second = (second.astype(F32) * factor).astype(BF16)
            mixed_re.append(second[0:64])
            mixed_im.append(second[64:128])
            for part in range(2):
                cot = cot_ref[2 * p + r, part]
                acc[part, 0:128, :] += dot32(first[:, 0:modes], cot)
                acc[part, 128:136, :] += jnp.broadcast_to(
                    jnp.sum(cot.astype(F32), axis=0, keepdims=True), (8, 64)
                )
        turned = (((1,), (1,)), ((), ()))
        grid = dot32(table[:, 0:wide], jnp.concatenate(mixed_re, axis=0), turned)
        grid = grid + dot32(table[:, wide : 2 * wide], jnp.concatenate(mixed_im, axis=0), turned)
        send2[p] = (grid * scale_t).astype(BF16).reshape(n, padded, 128)
        start_all(z_copy, send2, recv2, 1, p, n, me, 1)

    sums_send[0, 0:64, :] = acc[0, 0:64, :] + acc[1, 64:128, :]
    sums_send[0, 64:128, :] = acc[1, 0:64, :] - acc[0, 64:128, :]
    sums_send[0, 128:136, :] = acc[0, 128:136, :]
    sums_send[0, 136:144, :] = acc[1, 128:136, :]

    def sum_copy(i):
        axis, who = sum_steps[i]
        return pltpu.make_async_remote_copy(
            src_ref=sums_send.at[i],
            dst_ref=sums_recv.at[i],
            send_sem=s_send.at[i],
            recv_sem=s_recv.at[i],
            device_id={axis: who},
            device_id_type=MESH,
        )

    def finish_sum(i):
        sum_copy(i).wait()
        joined = sums_send[i] + sums_recv[i]
        if i + 1 < len(sum_steps):
            sums_send[i + 1] = joined
            sum_copy(i + 1).start()
        else:
            grad_ref[...] = joined

    early = len(sum_steps) // 2
    sum_copy(0).start()
    for i in range(early):
        finish_sum(i)

    for copy in weight_copies:
        copy.wait()

    lane_head = lax.broadcasted_iota(jnp.int32, (width, 128), 0) // hd
    pool = (lane_head == lax.broadcasted_iota(jnp.int32, (width, 128), 1)).astype(BF16)
    head_lane = lax.broadcasted_iota(jnp.int32, (128, width), 1) // hd
    spread_heads = (head_lane == lax.broadcasted_iota(jnp.int32, (128, width), 0)).astype(BF16)
    rows_all = nf * slab
    half_all = lanes_below((rows_all, 128), 64)
    groups = heads // kv_heads

    def head_norm(value, lanes):
        high, low = split_two(value * value)
        pooled = pool[0:lanes]
        mean = (dot32(high, pooled) + dot32(low, pooled)) * (1.0 / hd)
        high, low = split_two(lax.rsqrt(mean + 1e-06))
        wide_heads = spread_heads[:, 0:lanes]
        return value * (dot32(high, wide_heads) + dot32(low, wide_heads))

    def duplicate(value, ref):
        for j in range(kv_width // 128):
            part = value[:, j * 128 : (j + 1) * 128]
            rolled = pltpu.roll(part, 64, 1)
            ref[:, 2 * j * 128 : (2 * j + 1) * 128] = jnp.where(half_all, part, rolled)
            ref[:, (2 * j + 1) * 128 : (2 * j + 2) * 128] = jnp.where(half_all, rolled, part)

    def per_query_head(ref, t):
        rows = slice(t * slab, (t + 1) * slab)
        parts = []
        for kh in range(kv_heads):
            parts += [ref[rows, kh * 128 : (kh + 1) * 128]] * (groups // 2)
        return jnp.concatenate(parts, axis=1)

    @pl.loop(0, 2)
    def _(p):
        wait_recvs(z_copy, send2, recv2, 1, p, n, me, 1)
        for s in range(n // 2):
            lanes = slice(s * 128, (s + 1) * 128)
            even = recv2[p, 2 * s, 0:local, :].astype(F32)
            odd = recv2[p, 2 * s + 1, 0:local, :].astype(F32)
            grid_rows = (
                jnp.where(half, even, pltpu.roll(odd, 64, 1)),
                jnp.where(half, pltpu.roll(even, 64, 1), odd),
            )
            for r in range(2):
                inputs = fields_ref[2 * p + r, :, lanes].astype(F32) + embed_ref[2 * p + r, :, lanes]
                hidden = (inputs + grid_rows[r]).astype(BF16)
                first_slab = r * padded // slab
                for k in range(padded // slab):
                    count = min(slab, local - k * slab)
                    if count > 0:
                        sendh[p, first_slab + k, 0:count, lanes] = hidden[
                            k * slab : k * slab + count
                        ]
        start_all(f_copy, sendh, recvh, 0, p, nf, my_frame, 2)
        wait_recvs(f_copy, sendh, recvh, 0, p, nf, my_frame, 2)

        tokens = recvh[p].reshape(rows_all, width)
        query = head_norm(dot32(tokens, wq[...]), width)
        qs[...] = query.astype(BF16).astype(F32)
        keyval = dot32(tokens, wkv[...])
        keys = head_norm(keyval[:, 0:kv_width], kv_width)
        duplicate(keys.astype(BF16).astype(F32), kx)
        duplicate(keyval[:, kv_width:].astype(BF16).astype(F32), vx)
        top[...] = jnp.full_like(top, -3e38)
        first_seen = first_ref[0]
        for t in range(nf):
            rows = slice(t * slab, rows_all)
            count = nf - t
            product = (
                qs[rows, :].reshape(count, slab, width) * per_query_head(kx, t)[None]
            ).reshape(count * slab, width)
            high, low = split_two(product)
            score = (dot32(high, pool) + dot32(low, pool)) * scale_ref[...]
            if count > 1:
                later = jnp.where(t >= first_seen, score[slab:], -1e30)
                score = jnp.concatenate([score[0:slab], later], axis=0)
            scores[t, rows, :] = score
            top[rows, :] = jnp.maximum(top[rows, :], score)
        total[...] = jnp.zeros_like(total)
        for t in range(nf):
            rows = slice(t * slab, rows_all)
            weight = jnp.exp(scores[t, rows, :] - top[rows, :])
            scores[t, rows, :] = weight
            total[rows, :] += weight
        attended[...] = jnp.zeros_like(attended)
        for t in range(nf):
            rows = slice(t * slab, rows_all)
            count = nf - t
            probs = (scores[t, rows, :] / total[rows, :]).astype(BF16)
            spread_probs = dot32(probs, spread_heads)
            attended[rows, :] += (
                spread_probs.reshape(count, slab, width) * per_query_head(vx, t)[None]
            ).reshape(count * slab, width)
        output = dot32(attended[...].astype(BF16), wo[...])
        sendo[p] = (tokens.astype(F32) + output).astype(BF16).reshape(nf, slab, width)
        start_all(f_copy, sendo, recvo, 1, p, nf, my_frame, 3)

    for i in range(early, len(sum_steps)):
        finish_sum(i)

    @pl.loop(0, 2)
    def _(p):
        wait_recvs(f_copy, sendo, recvo, 1, p, nf, my_frame, 3)
        for r in range(2):
            first_slab = r * padded // slab
            for k in range(padded // slab):
                count = min(slab, local - k * slab)
                if count > 0:
                    out_ref[2 * p + r, k * slab : k * slab + count, :] = recvo[
                        p, first_slab + k, 0:count, :
                    ]

    @pl.loop(0, 2)
    def _(p):
        wait_sends(z_copy, send1, recv1, 0, p, n, me)
        wait_sends(z_copy, send2, recv2, 1, p, n, me)
        wait_sends(f_copy, sendh, recvh, 0, p, nf, my_frame)
        wait_sends(f_copy, sendo, recvo, 1, p, nf, my_frame)


def body(
    fields,
    band_rows,
    earliest_past_snapshot,
    lat_table,
    norm_gain,
    w_in1,
    b_in1,
    w_out2,
    b_out2,
    w_query,
    w_keyval,
    w_output,
    score_scale,
    spec_cot,
):
    _, _, lat_rows, local, width = fields.shape
    n = lax.axis_size("lon")
    nf = lax.axis_size("frame")
    nd = lax.axis_size("dp")
    modes = spec_cot.shape[4]
    block = w_in1.shape[2]
    heads = score_scale.shape[0]
    hd = width // heads
    kv_heads = w_keyval.shape[1] // 2 // hd
    padded = -(-local // 16) * 16
    wide = -(-modes // 128) * 128
    slab = 2 * padded // nf
    rows_all = 2 * padded
    geo = dict(
        lon=n,
        frame=nf,
        dp=nd,
        local=local,
        padded=padded,
        modes=modes,
        wide=wide,
        width=width,
        slab=slab,
        heads=heads,
        kv_heads=kv_heads,
        hd=hd,
    )
    near, far = angle_tables(local * n, local, n, padded, modes, wide)
    embed = lat_table[band_rows[0]].astype(F32).reshape(lat_rows, 1, width)
    scale_row = jnp.pad(score_scale / math.sqrt(hd), (0, 128 - heads)).reshape(1, 128)
    steps = int(math.log2(nd)) + int(math.log2(nf))
    vmem = pl.BlockSpec(memory_space=pltpu.VMEM)
    smem = pl.BlockSpec(memory_space=pltpu.SMEM)
    anywhere = pl.BlockSpec(memory_space=pl.ANY)
    out, grads = pl.pallas_call(
        functools.partial(layer_kernel, geo),
        out_shape=(
            jax.ShapeDtypeStruct((lat_rows, local, width), BF16),
            jax.ShapeDtypeStruct((144, block), F32),
        ),
        in_specs=[smem] + [vmem] * 11 + [anywhere] * 3,
        out_specs=(vmem, vmem),
        scratch_shapes=[
            pltpu.VMEM(w_query.shape, BF16),
            pltpu.VMEM(w_keyval.shape, BF16),
            pltpu.VMEM(w_output.shape, BF16),
            pltpu.VMEM((n * padded, 2 * wide), BF16),
            pltpu.VMEM((128, 128), BF16),
            pltpu.VMEM((128, 128), BF16),
            pltpu.VMEM((128, 128), F32),
        ]
        + [pltpu.VMEM((2, n, padded, 128), BF16)] * 4
        + [pltpu.VMEM((2, nf, slab, width), BF16)] * 4
        + [
            pltpu.VMEM((rows_all, width), F32),
            pltpu.VMEM((rows_all, kv_heads * 128), F32),
            pltpu.VMEM((rows_all, kv_heads * 128), F32),
            pltpu.VMEM((nf, rows_all, 128), F32),
            pltpu.VMEM((rows_all, 128), F32),
            pltpu.VMEM((rows_all, 128), F32),
            pltpu.VMEM((rows_all, width), F32),
            pltpu.VMEM((2, 136, block), F32),
            pltpu.VMEM((steps, 144, block), F32),
            pltpu.VMEM((steps, 144, block), F32),
            pltpu.SemaphoreType.DMA((3,)),
            pltpu.SemaphoreType.DMA((4, 2)),
            pltpu.SemaphoreType.DMA((2, 2, n)),
            pltpu.SemaphoreType.DMA((2, 2, n)),
            pltpu.SemaphoreType.DMA((2, 2, nf)),
            pltpu.SemaphoreType.DMA((2, 2, nf)),
            pltpu.SemaphoreType.DMA((steps,)),
            pltpu.SemaphoreType.DMA((steps,)),
        ],
        compiler_params=pltpu.CompilerParams(
            collective_id=0, has_side_effects=True, vmem_limit_bytes=60 * 2**20
        ),
        name="layer",
    )(
        earliest_past_snapshot,
        fields.reshape(lat_rows, local, width),
        embed,
        norm_gain.reshape(1, width),
        w_in1.reshape(2, block, block),
        b_in1,
        w_out2.reshape(2, block, block),
        b_out2,
        near,
        far,
        scale_row,
        spec_cot.reshape(lat_rows, 2, modes, block),
        w_query,
        w_keyval,
        w_output,
    )
    return (
        out.reshape(fields.shape),
        grads[0 : 2 * block].reshape(2, 1, block, block),
        jnp.stack([grads[2 * block], grads[2 * block + 8]]),
    )


def solution(mesh):
    placed = (
        P("dp", "frame", None, "lon", None),
        P("dp", None),
        P("dp"),
        P(),
        P(),
        P(None, "lon", None, None),
        P(None, "lon"),
        P(None, "lon", None, None),
        P(None, "lon"),
        P(),
        P(),
        P(),
        P(),
        P("dp", "frame", None, None, None, "lon"),
    )
    return jax.shard_map(
        body,
        mesh=mesh,
        in_specs=placed,
        out_specs=(P("dp", "frame", None, "lon", None), P(None, "lon", None, None), P(None, "lon")),
        check_vma=False,
    )
```

time: 600 us -> 164 us (0.27)
  the two profiles are of different devices: /device:TPU:1 before, /device:TPU:200 now
where the time goes in v1:
time: 164 us
  Pallas kernels  150 us (91%)
  local copies, waits for them, and re-layouts  10.8 us (7%)
  other arithmetic  1.89 us (1%)
    pallas_call x1, Pallas kernels, body(): pl.pallas_call(functools.partial(layer_kernel, geo), out_shape=(jax.Shape...  150 us
    unnamed x5, local copies, waits for them, and re-layouts  6.98 us

profile of v1, /device:TPU:200, one launch (start us, length us, event | category | flops | bytes accessed | tf_op | source)
XLA Modules:
  0.0 164.0 jit_solution(17399831867180978725)
XLA Ops:
  0.6 0.0 copy-start
  1.4 0.7 fusion
  2.1 0.7 broadcast_multiply_fusion
  2.7 0.5 pad_bitcast_fusion.scale_ref
  3.2 0.0 copy-done
  3.2 0.6 gather_fusion
  3.8 0.6 reshape.76.embed_ref
  4.4 2.2 %copy.20 = bf16[1,1,4,2,368,64]{5,4,3,2,1,0:T(8,128)(2,1)} copy(bf16[1,1,4,2,368,64]{4,5,3,2,1,0:T(8,128)(2,1)} %param.29) | data formatting | bytes 753664 | tf_op args[13]
  6.6 2.2 %copy.24 = bf16[1,1,4,90,1024]{4,3,2,1,0:T(8,128)(2,1)} copy(bf16[1,1,4,90,1024]{4,2,3,1,0:T(4,128)(2,1)} %param.16) | data formatting | bytes 1474560 | tf_op args[0]
  8.8 149.9 %layer.1 = (bf16[4,90,1024]{2,1,0:T(8,128)(2,1)}, f32[144,64]{1,0:T(8,128)}) custom-call(s32[1]{0:T(128)S(6)} %copy.25.first_ref, bf16[4,90,1024]{2,1,0:T(8,128)(2,1)} %bitcast.17, f32[4,1,1024]{2,1,0:T(1,128)} %reshape.76.embed_ref, f32[1,1024]{1,0:T(1,128)} %bitcast.23, bf16[2,64,64]{2,1,0:T(8,128)(2,1)} %bitcast.21, f32[2,64]{1,0:T(2,128)} %b1_ref.1, ...), custom_call_target="tpu_custom_call" | custom-call | tf_op jit(solution)/shard_map/layer/pallas_call | solution.py:469
  158.7 2.6 %copy.21 = bf16[1,1,4,90,1024]{4,2,3,1,0:T(4,128)(2,1)} copy(bf16[1,1,4,90,1024]{4,3,2,1,0:T(8,128)(2,1)} %bitcast.19) | data formatting | bytes 1474560
  161.3 0.7 fusion.1
  162.0 1.5 slice.9
  163.5 0.6 pad_maximum_fusion
  (1 shorter events, 0.0 us)
Async XLA Ops:
  0.6 2.6 %copy-start = (bf16[720,1024]{1,0:T(8,128)(2,1)S(1)}, bf16[720,1024]{1,0:T(8,128)(2,1)}, u32[]{:S(2)}) copy-start(bf16[720,1024]{1,0:T(8,128)(2,1)} %param.19) | copy-start | bytes 4423684

commit v2 on v1

v2 whole, which is shorter than its diff:
```python
import functools
import math

import jax
import jax.numpy as jnp
import numpy as np
from jax import lax
from jax.experimental import pallas as pl
from jax.experimental.pallas import tpu as pltpu
from jax.sharding import PartitionSpec as P

MESH = pl.DeviceIdType.MESH
EARLY = 3
F32 = jnp.float32
BF16 = jnp.bfloat16


def lanes_below(shape, bound):
    return lax.broadcasted_iota(jnp.int32, shape, len(shape) - 1) < bound


def split_two(value):
    high = value.astype(BF16)
    return high, (value - high.astype(F32)).astype(BF16)


def dot32(left, right, dims=(((1,), (0,)), ((), ()))):
    return lax.dot_general(left, right, dims, preferred_element_type=F32)


def angle_tables(length, local, parts, padded, modes, wide):
    near = np.zeros((2, padded, wide), np.float64)
    far = np.zeros((2, parts, 1, wide), np.float64)
    wave = np.arange(modes)
    turn = 2.0 * np.pi / length
    inner = (np.arange(local)[:, None] * wave[None, :]) % length
    near[0, :local, :modes] = np.cos(turn * inner)
    near[1, :local, :modes] = np.sin(turn * inner)
    outer = (np.arange(parts)[:, None] * local * wave[None, :]) % length
    far[0, :, 0, :modes] = np.cos(turn * outer)
    far[1, :, 0, :modes] = np.sin(turn * outer)
    return near.astype(np.float32), far.astype(np.float32)


def layer_kernel(
    geo,
    first_ref,
    band_ref,
    heads_ref,
    fields_ref,
    lat_ref,
    gain_ref,
    w1_ref,
    b1_ref,
    w2_ref,
    b2_ref,
    near_ref,
    far_ref,
    cot_ref,
    wq_hbm,
    wkv_hbm,
    wo_hbm,
    out_ref,
    grad_ref,
    bias_ref,
    embed,
    wq,
    wkv,
    wo,
    table,
    mix1,
    mix2,
    brow,
    send1,
    recv1,
    send2,
    recv2,
    sendh_a,
    recvh_a,
    sendo_a,
    recvo_a,
    sendh_b,
    recvh_b,
    sendo_b,
    recvo_b,
    qs,
    kx,
    vx,
    scores,
    top,
    total,
    attended,
    acc,
    bias_acc,
    sums_send,
    sums_recv,
    weight_sem,
    own_z_sem,
    own_f_sem,
    z_send,
    z_recv,
    f_send,
    f_recv,
    s_send,
    s_recv,
):
    n, nf, nd = geo["lon"], geo["frame"], geo["dp"]
    local, padded, modes, wide = geo["local"], geo["padded"], geo["modes"], geo["wide"]
    width, pieces = geo["width"], geo["pieces"]
    heads, kv_heads, hd = geo["heads"], geo["kv_heads"], geo["hd"]
    kv_width = kv_heads * hd
    sendh, recvh = (sendh_a, sendh_b), (recvh_a, recvh_b)
    sendo, recvo = (sendo_a, sendo_b), (recvo_a, recvo_b)
    scale_t = 1.0 / math.sqrt(local * n)
    me = lax.axis_index("lon")
    my_frame = lax.axis_index("frame")
    my_dp = lax.axis_index("dp")

    def partner(index, bit):
        return index + bit * (1 - 2 * ((index // bit) % 2))

    sum_steps = []
    bit = 1
    while bit < nd:
        sum_steps.append(("dp", partner(my_dp, bit)))
        bit *= 2
    bit = 1
    while bit < nf:
        sum_steps.append(("frame", partner(my_frame, bit)))
        bit *= 2
    dp_partners = [who for axis, who in sum_steps if axis == "dp"]

    barrier = pltpu.get_barrier_semaphore()

    @pl.loop(1, n)
    def _(o):
        pl.semaphore_signal(
            barrier, inc=1, device_id={"lon": lax.rem(me + o, n)}, device_id_type=MESH
        )

    @pl.loop(1, nf)
    def _(o):
        pl.semaphore_signal(
            barrier, inc=1, device_id={"frame": lax.rem(my_frame + o, nf)}, device_id_type=MESH
        )

    for who in dp_partners:
        pl.semaphore_signal(barrier, inc=1, device_id={"dp": who}, device_id_type=MESH)

    weight_copies = [
        pltpu.make_async_copy(src, dst, weight_sem.at[i])
        for i, (src, dst) in enumerate(((wq_hbm, wq), (wkv_hbm, wkv), (wo_hbm, wo)))
    ]
    for copy in weight_copies:
        copy.start()

    rows_in = lat_ref.shape[0]
    picked = jnp.full((8, rows_in), band_ref[0, 0], jnp.int32)
    sublane = lax.broadcasted_iota(jnp.int32, (8, rows_in), 0)
    for r in range(1, band_ref.shape[1]):
        picked = jnp.where(sublane == r, band_ref[0, r], picked)
    onehot = (lax.broadcasted_iota(jnp.int32, (8, rows_in), 1) == picked).astype(BF16)
    looked_up = dot32(onehot, lat_ref[...])
    for r in range(band_ref.shape[1]):
        embed[r] = looked_up[r : r + 1]

    tail = local // 16 * 16
    send1[:, :, tail:, :] = jnp.zeros((2, n, padded - tail, 128), BF16)
    for piece, (start, span) in enumerate(pieces):
        slab = 2 * span // nf
        for k in range(nf // 2):
            if local - start - k * slab < slab:
                used = max(0, (local - start - k * slab) // 8 * 8)
                for r in range(2):
                    sendh[piece][:, r * nf // 2 + k, used:, :] = jnp.zeros(
                        (2, slab - used, width), BF16
                    )

    peers = n - 1

    def z_offset(i):
        return n // 2 + (i % 2) * ((i + 1) // 2) - (1 - i % 2) * (i // 2)

    def z_copy(src, dst, group, p, rows, i, target, slot):
        return pltpu.make_async_remote_copy(
            src_ref=src.at[p, target, rows],
            dst_ref=dst.at[p, slot, rows],
            send_sem=z_send.at[group, i],
            recv_sem=z_recv.at[group, i],
            device_id={"lon": target},
            device_id_type=MESH,
        )

    def z_own(src, dst, group, p, rows):
        return pltpu.make_async_copy(
            src.at[p, me, rows], dst.at[p, me, rows], own_z_sem.at[group]
        )

    def z_start(src, dst, group, p, rows):
        @pl.loop(0, peers)
        def _(i):
            target = lax.rem(me + z_offset(i), n)
            z_copy(src, dst, group, p, rows, i, target, me).start()

        z_own(src, dst, group, p, rows).start()

    def z_wait(src, dst, group, p, rows):
        z_own(src, dst, group, p, rows).wait()

        @pl.loop(0, peers)
        def _(i):
            peer = lax.rem(me + n - z_offset(i), n)
            z_copy(src, dst, group, p, rows, i, peer, peer).wait_recv()

    def z_sent(src, dst, group, p, rows):
        @pl.loop(0, peers)
        def _(i):
            target = lax.rem(me + z_offset(i), n)
            z_copy(src, dst, group, p, rows, i, target, me).wait_send()

    whole = pl.ds(0, padded)
    chunks = [(p, piece) for p in range(2) for piece in range(len(pieces))]

    def back_args(c):
        p, piece = chunks[c]
        return send2, recv2, 2 + c, p, pl.ds(*pieces[piece])

    def f_copy(src, dst, group, p, o, target, slot):
        return pltpu.make_async_remote_copy(
            src_ref=src.at[p, target],
            dst_ref=dst.at[p, slot],
            send_sem=f_send.at[group, o],
            recv_sem=f_recv.at[group, o],
            device_id={"frame": target},
            device_id_type=MESH,
        )

    def f_own(src, dst, group, p):
        return pltpu.make_async_copy(
            src.at[p, my_frame], dst.at[p, my_frame], own_f_sem.at[group]
        )

    def f_start(src, dst, group, p):
        @pl.loop(1, nf)
        def _(o):
            f_copy(src, dst, group, p, o, lax.rem(my_frame + o, nf), my_frame).start()

        f_own(src, dst, group, p).start()

    def f_wait(src, dst, group, p):
        f_own(src, dst, group, p).wait()

        @pl.loop(1, nf)
        def _(o):
            peer = lax.rem(my_frame + nf - o, nf)
            f_copy(src, dst, group, p, o, peer, peer).wait_recv()

    def f_sent(src, dst, group, p):
        @pl.loop(1, nf)
        def _(o):
            f_copy(src, dst, group, p, o, lax.rem(my_frame + o, nf), my_frame).wait_send()

    def out_args(c):
        p, piece = chunks[c]
        return sendh[piece], recvh[piece], 2 * c, p

    def home_args(c):
        p, piece = chunks[c]
        return sendo[piece], recvo[piece], 2 * c + 1, p

    half = lanes_below((local, 128), 64)

    def normalize(p, r):
        cells = fields_ref[2 * p + r].astype(F32) + embed[2 * p + r]
        cells = cells - jnp.mean(cells, axis=-1, keepdims=True)
        spread = jnp.mean(cells * cells, axis=-1, keepdims=True)
        return cells * lax.rsqrt(spread + 1e-05) * gain_ref[...]

    def fill(p):
        row_a = normalize(p, 0)
        row_b = normalize(p, 1)
        for s in range(n // 2):
            part_a = row_a[:, s * 128 : (s + 1) * 128]
            part_b = row_b[:, s * 128 : (s + 1) * 128]
            even = jnp.where(half, part_a, pltpu.roll(part_b, 64, 1))
            odd = jnp.where(half, pltpu.roll(part_a, 64, 1), part_b)
            send1[p, 2 * s, 0:local, :] = even.astype(BF16)
            send1[p, 2 * s + 1, 0:local, :] = odd.astype(BF16)

    fill(0)
    pl.semaphore_wait(barrier, (n - 1) + (nf - 1) + len(dp_partners))
    z_start(send1, recv1, 0, 0, whole)
    fill(1)
    z_start(send1, recv1, 1, 1, whole)

    near_cos, near_sin = near_ref[0], near_ref[1]

    @pl.loop(0, n)
    def _(s):
        far_cos, far_sin = far_ref[0, s], far_ref[1, s]
        rows = pl.ds(pl.multiple_of(s * padded, padded), padded)
        table[rows, 0:wide] = (near_cos * far_cos - near_sin * far_sin).astype(BF16)
        table[rows, wide : 2 * wide] = (-(near_sin * far_cos + near_cos * far_sin)).astype(BF16)

    columns = []
    for w_ref, mix, b_ref in ((w1_ref, mix1, b1_ref), (w2_ref, mix2, b2_ref)):
        brow[0:64, 0:64] = w_ref[0].astype(F32)
        brow[0:64, 64:128] = w_ref[1].astype(F32)
        brow[64:128, 0:64] = -w_ref[1].astype(F32)
        brow[64:128, 64:128] = w_ref[0].astype(F32)
        mix[...] = brow[...].T.astype(BF16)
        brow[0:1, 0:64] = b_ref[0:1, :]
        brow[0:1, 64:128] = b_ref[1:2, :]
        columns.append(jnp.broadcast_to(brow[0:1, :], (128, 128)).T[:, 0:1])
    column1, column2 = columns
    wave = lax.broadcasted_iota(jnp.int32, (128, wide), 1)
    factor = jnp.where(wave == 0, 1.0, 2.0)

    turned = (((1,), (1,)), ((), ()))
    acc[...] = jnp.zeros_like(acc)
    bias_acc[...] = jnp.zeros_like(bias_acc)

    def transform(p):
        z_wait(send1, recv1, p, p, whole)
        gathered = recv1[p].reshape(n * padded, 128)
        spectrum = dot32(gathered.T, table[...]) * scale_t
        cos_part = spectrum[:, 0:wide].astype(BF16)
        sin_part = spectrum[:, wide : 2 * wide].astype(BF16)
        mixed_re, mixed_im = [], []
        for r in range(2):
            stacked = jnp.concatenate(
                [cos_part[64 * r : 64 * r + 64], sin_part[64 * r : 64 * r + 64]], axis=0
            )
            first = jnp.maximum(dot32(mix1[...], stacked) + column1, 0.0).astype(BF16)
            second = (dot32(mix2[...], first) + column2).astype(BF16)
            second = (second.astype(F32) * factor).astype(BF16)
            mixed_re.append(second[0:64])
            mixed_im.append(second[64:128])
            for part in range(2):
                cot = cot_ref[2 * p + r, part]
                acc[part, 0:128, :] += dot32(first[:, 0:modes], cot, turned)
                bias_acc[part] += jnp.broadcast_to(
                    jnp.sum(cot.astype(F32), axis=1, keepdims=True), (64, 128)
                )
        grid = dot32(table[:, 0:wide], jnp.concatenate(mixed_re, axis=0), turned)
        grid = grid + dot32(table[:, wide : 2 * wide], jnp.concatenate(mixed_im, axis=0), turned)
        send2[p] = (grid * scale_t).astype(BF16).reshape(n, padded, 128)
        for c in range(len(chunks)):
            if chunks[c][0] == p:
                z_start(*back_args(c))

    transform(0)
    transform(1)

    sums_send[0, 0:64, :] = acc[0, 0:64, :] + acc[1, 64:128, :]
    sums_send[0, 64:128, :] = acc[1, 0:64, :] - acc[0, 64:128, :]
    for part in range(2):
        sums_send[0, 128 + 8 * part : 136 + 8 * part, :] = bias_acc[part].T[0:8, :]

    def sum_copy(i):
        axis, who = sum_steps[i]
        return pltpu.make_async_remote_copy(
            src_ref=sums_send.at[i],
            dst_ref=sums_recv.at[i],
            send_sem=s_send.at[i],
            recv_sem=s_recv.at[i],
            device_id={axis: who},
            device_id_type=MESH,
        )

    def finish_sum(i):
        sum_copy(i).wait()
        joined = sums_send[i] + sums_recv[i]
        if i + 1 < len(sum_steps):
            sums_send[i + 1] = joined
            sum_copy(i + 1).start()
        else:
            grad_ref[...] = joined[0:128]
            bias_ref[0:1, :] = joined[128:129]
            bias_ref[1:2, :] = joined[136:137]

    sum_copy(0).start()
    steps = len(sum_steps)
    early = min(EARLY, steps)
    for i in range(early):
        finish_sum(i)

    for copy in weight_copies:
        copy.wait()

    lane_head = lax.broadcasted_iota(jnp.int32, (width, 128), 0) // hd
    pool = (lane_head == lax.broadcasted_iota(jnp.int32, (width, 128), 1)).astype(BF16)
    head_lane = lax.broadcasted_iota(jnp.int32, (128, width), 1) // hd
    spread_heads = (head_lane == lax.broadcasted_iota(jnp.int32, (128, width), 0)).astype(BF16)
    head_ids = lax.broadcasted_iota(jnp.int32, (1, 128), 1)
    score_row = jnp.zeros((1, 128), F32)
    for h in range(heads):
        score_row = jnp.where(head_ids == h, heads_ref[h] * (1.0 / math.sqrt(hd)), score_row)
    groups = heads // kv_heads

    def head_norm(value, lanes):
        high, low = split_two(value * value)
        pooled = pool[0:lanes]
        mean = (dot32(high, pooled) + dot32(low, pooled)) * (1.0 / hd)
        high, low = split_two(lax.rsqrt(mean + 1e-06))
        wide_heads = spread_heads[:, 0:lanes]
        return value * (dot32(high, wide_heads) + dot32(low, wide_heads))

    def duplicate(value, ref):
        rows_all = value.shape[0]
        half_all = lanes_below((rows_all, 128), 64)
        for j in range(kv_width // 128):
            part = value[:, j * 128 : (j + 1) * 128]
            rolled = pltpu.roll(part, 64, 1)
            ref[0:rows_all, 2 * j * 128 : (2 * j + 1) * 128] = jnp.where(half_all, part, rolled)
            ref[0:rows_all, (2 * j + 1) * 128 : (2 * j + 2) * 128] = jnp.where(half_all, rolled, part)

    def per_query_head(ref, t, slab):
        rows = slice(t * slab, (t + 1) * slab)
        parts = []
        for kh in range(kv_heads):
            parts += [ref[rows, kh * 128 : (kh + 1) * 128]] * (groups // 2)
        return jnp.concatenate(parts, axis=1)

    def exchange(c):
        p, piece = chunks[c]
        start, span = pieces[piece]
        slab = 2 * span // nf
        z_wait(*back_args(c))
        count = min(span, local - start)
        near_half = lanes_below((count, 128), 64)
        for s in range(n // 2):
            lanes = slice(s * 128, (s + 1) * 128)
            even = recv2[p, 2 * s, start : start + count, :].astype(F32)
            odd = recv2[p, 2 * s + 1, start : start + count, :].astype(F32)
            grid_rows = (
                jnp.where(near_half, even, pltpu.roll(odd, 64, 1)),
                jnp.where(near_half, pltpu.roll(even, 64, 1), odd),
            )
            for r in range(2):
                inputs = fields_ref[2 * p + r, start : start + count, lanes].astype(F32)
                inputs = inputs + embed[2 * p + r, :, lanes]
                hidden = (inputs + grid_rows[r]).astype(BF16)
                for k in range(nf // 2):
                    used = min(slab, count - k * slab)
                    if used > 0:
                        sendh[piece][p, r * nf // 2 + k, 0:used, lanes] = hidden[
                            k * slab : k * slab + used
                        ]
        f_start(*out_args(c))

    def attend(c):
        p, piece = chunks[c]
        slab = 2 * pieces[piece][1] // nf
        rows_all = nf * slab
        every = slice(0, rows_all)
        f_wait(*out_args(c))
        tokens = recvh[piece][p].reshape(rows_all, width)
        query = head_norm(dot32(tokens, wq[...]), width)
        qs[every, :] = query.astype(BF16).astype(F32)
        keyval = dot32(tokens, wkv[...])
        keys = head_norm(keyval[:, 0:kv_width], kv_width)
        duplicate(keys.astype(BF16).astype(F32), kx)
        duplicate(keyval[:, kv_width:].astype(BF16).astype(F32), vx)
        top[every, :] = jnp.full((rows_all, 128), -3e38, F32)
        first_seen = first_ref[0]
        for t in range(nf):
            rows = slice(t * slab, rows_all)
            count = nf - t
            product = (
                qs[rows, :].reshape(count, slab, width) * per_query_head(kx, t, slab)[None]
            ).reshape(count * slab, width)
            high, low = split_two(product)
            score = (dot32(high, pool) + dot32(low, pool)) * score_row
            if count > 1:
                later = jnp.where(t >= first_seen, score[slab:], -1e30)
                score = jnp.concatenate([score[0:slab], later], axis=0)
            scores[t, rows, :] = score
            top[rows, :] = jnp.maximum(top[rows, :], score)
        total[every, :] = jnp.zeros((rows_all, 128), F32)
        for t in range(nf):
            rows = slice(t * slab, rows_all)
            weight = jnp.exp(scores[t, rows, :] - top[rows, :])
            scores[t, rows, :] = weight
            total[rows, :] += weight
        attended[every, :] = jnp.zeros((rows_all, width), F32)
        for t in range(nf):
            rows = slice(t * slab, rows_all)
            count = nf - t
            probs = (scores[t, rows, :] / total[rows, :]).astype(BF16)
            spread_probs = dot32(probs, spread_heads)
            attended[rows, :] += (
                spread_probs.reshape(count, slab, width) * per_query_head(vx, t, slab)[None]
            ).reshape(count * slab, width)
        output = dot32(attended[every, :].astype(BF16), wo[...])
        sendo[piece][p] = (tokens.astype(F32) + output).astype(BF16).reshape(nf, slab, width)
        f_start(*home_args(c))

    pending = list(range(early, steps))

    def next_sum():
        if pending:
            finish_sum(pending.pop(0))

    last = len(chunks)
    exchange(0)
    next_sum()
    for c in range(1, last):
        exchange(c)
        if c == 1:
            next_sum()
        attend(c - 1)
    attend(last - 1)
    while pending:
        next_sum()

    for c in range(last):
        p, piece = chunks[c]
        start, span = pieces[piece]
        slab = 2 * span // nf
        f_wait(*home_args(c))
        for r in range(2):
            for k in range(nf // 2):
                first = start + k * slab
                used = min(slab, local - first)
                if used > 0:
                    out_ref[2 * p + r, first : first + used, :] = recvo[piece][
                        p, r * nf // 2 + k, 0:used, :
                    ]

    for p in range(2):
        z_sent(send1, recv1, p, p, whole)
    for c in range(last):
        z_sent(*back_args(c))
        f_sent(*out_args(c))
        f_sent(*home_args(c))


def body(
    fields,
    band_rows,
    earliest_past_snapshot,
    lat_table,
    norm_gain,
    w_in1,
    b_in1,
    w_out2,
    b_out2,
    w_query,
    w_keyval,
    w_output,
    score_scale,
    spec_cot,
):
    _, _, lat_rows, local, width = fields.shape
    n = lax.axis_size("lon")
    nf = lax.axis_size("frame")
    nd = lax.axis_size("dp")
    modes = spec_cot.shape[4]
    block = w_in1.shape[2]
    heads = score_scale.shape[0]
    hd = width // heads
    kv_heads = w_keyval.shape[1] // 2 // hd
    padded = -(-local // 16) * 16
    wide = -(-modes // 128) * 128
    units = 2 * padded // nf // 8
    split = (units + 1) // 2 * 4 * nf
    pieces = ((0, split), (split, padded - split))
    rows_all = 2 * split
    geo = dict(
        lon=n,
        frame=nf,
        dp=nd,
        local=local,
        padded=padded,
        modes=modes,
        wide=wide,
        width=width,
        pieces=pieces,
        heads=heads,
        kv_heads=kv_heads,
        hd=hd,
    )
    near, far = angle_tables(local * n, local, n, padded, modes, wide)
    steps = int(math.log2(nd)) + int(math.log2(nf))
    vmem = pl.BlockSpec(memory_space=pltpu.VMEM)
    smem = pl.BlockSpec(memory_space=pltpu.SMEM)
    anywhere = pl.BlockSpec(memory_space=pl.ANY)
    out, grads, bias = pl.pallas_call(
        functools.partial(layer_kernel, geo),
        out_shape=(
            jax.ShapeDtypeStruct((lat_rows, local, width), BF16),
            jax.ShapeDtypeStruct((2 * block, block), F32),
            jax.ShapeDtypeStruct((2, block), F32),
        ),
        in_specs=[smem] * 3 + [vmem] * 10 + [anywhere] * 3,
        out_specs=(vmem, vmem, vmem),
        scratch_shapes=[
            pltpu.VMEM((lat_rows, 1, width), F32),
            pltpu.VMEM(w_query.shape, BF16),
            pltpu.VMEM(w_keyval.shape, BF16),
            pltpu.VMEM(w_output.shape, BF16),
            pltpu.VMEM((n * padded, 2 * wide), BF16),
            pltpu.VMEM((128, 128), BF16),
            pltpu.VMEM((128, 128), BF16),
            pltpu.VMEM((128, 128), F32),
        ]
        + [pltpu.VMEM((2, n, padded, 128), BF16)] * 4
        + [pltpu.VMEM((2, nf, 2 * pieces[0][1] // nf, width), BF16)] * 4
        + [pltpu.VMEM((2, nf, 2 * pieces[1][1] // nf, width), BF16)] * 4
        + [
            pltpu.VMEM((rows_all, width), F32),
            pltpu.VMEM((rows_all, kv_heads * 128), F32),
            pltpu.VMEM((rows_all, kv_heads * 128), F32),
            pltpu.VMEM((nf, rows_all, 128), F32),
            pltpu.VMEM((rows_all, 128), F32),
            pltpu.VMEM((rows_all, 128), F32),
            pltpu.VMEM((rows_all, width), F32),
            pltpu.VMEM((2, 128, block), F32),
            pltpu.VMEM((2, block, 128), F32),
            pltpu.VMEM((steps, 144, block), F32),
            pltpu.VMEM((steps, 144, block), F32),
            pltpu.SemaphoreType.DMA((3,)),
            pltpu.SemaphoreType.DMA((6,)),
            pltpu.SemaphoreType.DMA((8,)),
            pltpu.SemaphoreType.DMA((6, n - 1)),
            pltpu.SemaphoreType.DMA((6, n - 1)),
            pltpu.SemaphoreType.DMA((8, nf)),
            pltpu.SemaphoreType.DMA((8, nf)),
            pltpu.SemaphoreType.DMA((steps,)),
            pltpu.SemaphoreType.DMA((steps,)),
        ],
        compiler_params=pltpu.CompilerParams(
            collective_id=0, has_side_effects=True, vmem_limit_bytes=60 * 2**20
        ),
        name="layer",
    )(
        earliest_past_snapshot,
        band_rows,
        score_scale,
        fields.reshape(lat_rows, local, width),
        lat_table,
        norm_gain.reshape(1, width),
        w_in1.reshape(2, block, block),
        b_in1,
        w_out2.reshape(2, block, block),
        b_out2,
        near,
        far,
        spec_cot.reshape(lat_rows, 2, modes, block).transpose(0, 1, 3, 2),
        w_query,
        w_keyval,
        w_output,
    )
    return (
        out.reshape(fields.shape),
        grads.reshape(2, 1, block, block),
        bias,
    )


def solution(mesh):
    placed = (
        P("dp", "frame", None, "lon", None),
        P("dp", None),
        P("dp"),
        P(),
        P(),
        P(None, "lon", None, None),
        P(None, "lon"),
        P(None, "lon", None, None),
        P(None, "lon"),
        P(),
        P(),
        P(),
        P(),
        P("dp", "frame", None, None, None, "lon"),
    )
    return jax.shard_map(
        body,
        mesh=mesh,
        in_specs=placed,
        out_specs=(P("dp", "frame", None, "lon", None), P(None, "lon", None, None), P(None, "lon")),
        check_vma=False,
    )
```

time: 164 us -> 148 us (0.902)
  the two profiles are of different devices: /device:TPU:200 before, /device:TPU:136 now
where the time goes in v2:
time: 148 us; the launch traced here: 147 us
  Pallas kernels  138 us (93%)
  local copies, waits for them, and re-layouts  7.52 us (5%)
    pallas_call x1, Pallas kernels, body(): pl.pallas_call(functools.partial(layer_kernel, geo), out_shape=(jax.Shape...  138 us
    unnamed x4, local copies, waits for them, and re-layouts  7.52 us

profile of v2, /device:TPU:136, one launch (start us, length us, event | category | flops | bytes accessed | tf_op | source)
XLA Modules:
  0.0 147.2 jit_solution(12396331045802310572)
XLA Ops:
  1.3 2.2 %copy.23 = bf16[1,1,4,90,1024]{4,3,2,1,0:T(8,128)(2,1)} copy(bf16[1,1,4,90,1024]{4,2,3,1,0:T(4,128)(2,1)} %param.16) | data formatting | bytes 1474560 | tf_op args[0]
  3.5 138.4 %layer.1 = (bf16[4,90,1024]{2,1,0:T(8,128)(2,1)}, f32[128,64]{1,0:T(8,128)}, f32[2,64]{1,0:T(2,128)}) custom-call(s32[1]{0:T(128)S(6)} %copy.26.first_ref, s32[1,4]{1,0:T(1,128)} %band_ref.1, f32[16]{0:T(128)} %heads_ref.1, bf16[4,90,1024]{2,1,0:T(8,128)(2,1)} %bitcast.13, bf16[720,1024]{1,0:T(8,128)(2,1)} %lat_ref.1, f32[1,1024]{1,0:T(1,128)} %bitcast.19, ...), custom_call_target="tpu_custom_call" | custom-call | tf_op jit(solution)/shard_map/layer/pallas_call | solution.py:589
  141.9 2.6 %copy.20 = bf16[1,1,4,90,1024]{4,2,3,1,0:T(4,128)(2,1)} copy(bf16[1,1,4,90,1024]{4,3,2,1,0:T(8,128)(2,1)} %bitcast.14) | data formatting | bytes 1474560
  144.5 1.5 %copy.27 = f32[2,1,64,64]{3,2,1,0:T(8,128)} copy(f32[2,1,64,64]{3,2,1,0:T(8,128)} %bitcast.16) | data formatting | bytes 65536
  146.0 1.2 copy.28

commit v3 on v2

--- a/solution.py
+++ b/solution.py
@@ -83,6 +83,8 @@
     recvh_b,
     sendo_b,
     recvo_b,
+    sendkv,
+    recvkv,
     qs,
     kx,
     vx,
@@ -97,6 +99,8 @@
     weight_sem,
     own_z_sem,
     own_f_sem,
+    kv_send,
+    kv_recv,
     z_send,
     z_recv,
     f_send,
@@ -115,6 +119,9 @@
     me = lax.axis_index("lon")
     my_frame = lax.axis_index("frame")
     my_dp = lax.axis_index("dp")
+    nx = nf // 2
+    my_x, side = my_frame // 2, lax.rem(my_frame, 2)
+    other_side = my_x * 2 + 1 - side
 
     def partner(index, bit):
         return index + bit * (1 - 2 * ((index // bit) % 2))
@@ -138,11 +145,16 @@
             barrier, inc=1, device_id={"lon": lax.rem(me + o, n)}, device_id_type=MESH
         )
 
-    @pl.loop(1, nf)
+    @pl.loop(1, nx)
     def _(o):
         pl.semaphore_signal(
-            barrier, inc=1, device_id={"frame": lax.rem(my_frame + o, nf)}, device_id_type=MESH
+            barrier,
+            inc=1,
+            device_id={"frame": lax.rem(my_x + o, nx) * 2 + side},
+            device_id_type=MESH,
         )
+
+    pl.semaphore_signal(barrier, inc=1, device_id={"frame": other_side}, device_id_type=MESH)
 
     for who in dp_partners:
         pl.semaphore_signal(barrier, inc=1, device_id={"dp": who}, device_id_type=MESH)
@@ -167,12 +179,12 @@
     tail = local // 16 * 16
     send1[:, :, tail:, :] = jnp.zeros((2, n, padded - tail, 128), BF16)
     for piece, (start, span) in enumerate(pieces):
-        slab = 2 * span // nf
-        for k in range(nf // 2):
+        slab = 2 * span // nx
+        for k in range(nx // 2):
             if local - start - k * slab < slab:
                 used = max(0, (local - start - k * slab) // 8 * 8)
                 for r in range(2):
-                    sendh[piece][:, r * nf // 2 + k, used:, :] = jnp.zeros(
+                    sendh[piece][:, r * nx // 2 + k, used:, :] = jnp.zeros(
                         (2, slab - used, width), BF16
                     )
 
@@ -231,34 +243,43 @@
             dst_ref=dst.at[p, slot],
             send_sem=f_send.at[group, o],
             recv_sem=f_recv.at[group, o],
-            device_id={"frame": target},
+            device_id={"frame": target * 2 + side},
             device_id_type=MESH,
         )
 
     def f_own(src, dst, group, p):
-        return pltpu.make_async_copy(
-            src.at[p, my_frame], dst.at[p, my_frame], own_f_sem.at[group]
-        )
+        return pltpu.make_async_copy(src.at[p, my_x], dst.at[p, my_x], own_f_sem.at[group])
 
     def f_start(src, dst, group, p):
-        @pl.loop(1, nf)
+        @pl.loop(1, nx)
         def _(o):
-            f_copy(src, dst, group, p, o, lax.rem(my_frame + o, nf), my_frame).start()
+            f_copy(src, dst, group, p, o, lax.rem(my_x + o, nx), my_x).start()
 
         f_own(src, dst, group, p).start()
 
     def f_wait(src, dst, group, p):
         f_own(src, dst, group, p).wait()
 
-        @pl.loop(1, nf)
+        @pl.loop(1, nx)
         def _(o):
-            peer = lax.rem(my_frame + nf - o, nf)
+            peer = lax.rem(my_x + nx - o, nx)
             f_copy(src, dst, group, p, o, peer, peer).wait_recv()
 
     def f_sent(src, dst, group, p):
-        @pl.loop(1, nf)
+        @pl.loop(1, nx)
         def _(o):
-            f_copy(src, dst, group, p, o, lax.rem(my_frame + o, nf), my_frame).wait_send()
+            f_copy(src, dst, group, p, o, lax.rem(my_x + o, nx), my_x).wait_send()
+
+    def kv_copy(c):
+        rows = pl.ds(0, 2 * pieces[chunks[c][1]][1])
+        return pltpu.make_async_remote_copy(
+            src_ref=sendkv.at[c, rows],
+            dst_ref=recvkv.at[c, rows],
+            send_sem=kv_send.at[c],
+            recv_sem=kv_recv.at[c],
+            device_id={"frame": other_side},
+            device_id_type=MESH,
+        )
 
     def out_args(c):
         p, piece = chunks[c]
@@ -288,7 +309,7 @@
             send1[p, 2 * s + 1, 0:local, :] = odd.astype(BF16)
 
     fill(0)
-    pl.semaphore_wait(barrier, (n - 1) + (nf - 1) + len(dp_partners))
+    pl.semaphore_wait(barrier, (n - 1) + nx + len(dp_partners))
     z_start(send1, recv1, 0, 0, whole)
     fill(1)
     z_start(send1, recv1, 1, 1, whole)
@@ -406,26 +427,29 @@
         wide_heads = spread_heads[:, 0:lanes]
         return value * (dot32(high, wide_heads) + dot32(low, wide_heads))
 
-    def duplicate(value, ref):
+    def duplicate(value, ref, slot, half_id):
         rows_all = value.shape[0]
         half_all = lanes_below((rows_all, 128), 64)
         for j in range(kv_width // 128):
             part = value[:, j * 128 : (j + 1) * 128]
             rolled = pltpu.roll(part, 64, 1)
-            ref[0:rows_all, 2 * j * 128 : (2 * j + 1) * 128] = jnp.where(half_all, part, rolled)
-            ref[0:rows_all, (2 * j + 1) * 128 : (2 * j + 2) * 128] = jnp.where(half_all, rolled, part)
-
-    def per_query_head(ref, t, slab):
+            low, high = slice(2 * j * 128, (2 * j + 1) * 128), slice(
+                (2 * j + 1) * 128, (2 * j + 2) * 128
+            )
+            ref[slot, half_id, 0:rows_all, low] = jnp.where(half_all, part, rolled)
+            ref[slot, half_id, 0:rows_all, high] = jnp.where(half_all, rolled, part)
+
+    def per_query_head(ref, slot, half_id, t, slab):
         rows = slice(t * slab, (t + 1) * slab)
         parts = []
         for kh in range(kv_heads):
-            parts += [ref[rows, kh * 128 : (kh + 1) * 128]] * (groups // 2)
+            parts += [ref[slot, half_id, rows, kh * 128 : (kh + 1) * 128]] * (groups // 2)
         return jnp.concatenate(parts, axis=1)
 
     def exchange(c):
         p, piece = chunks[c]
         start, span = pieces[piece]
-        slab = 2 * span // nf
+        slab = 2 * span // nx
         z_wait(*back_args(c))
         count = min(span, local - start)
         near_half = lanes_below((count, 128), 64)
@@ -441,59 +465,92 @@
                 inputs = fields_ref[2 * p + r, start : start + count, lanes].astype(F32)
                 inputs = inputs + embed[2 * p + r, :, lanes]
                 hidden = (inputs + grid_rows[r]).astype(BF16)
-                for k in range(nf // 2):
+                for k in range(nx // 2):
                     used = min(slab, count - k * slab)
                     if used > 0:
-                        sendh[piece][p, r * nf // 2 + k, 0:used, lanes] = hidden[
+                        sendh[piece][p, r * nx // 2 + k, 0:used, lanes] = hidden[
                             k * slab : k * slab + used
                         ]
         f_start(*out_args(c))
 
-    def attend(c):
+    first_seen = first_ref[0]
+
+    def project(c):
         p, piece = chunks[c]
-        slab = 2 * pieces[piece][1] // nf
-        rows_all = nf * slab
+        rows_all = 2 * pieces[piece][1]
         every = slice(0, rows_all)
+        slot = c % 2
         f_wait(*out_args(c))
         tokens = recvh[piece][p].reshape(rows_all, width)
+        keyval = dot32(tokens, wkv[...])
+        keys = head_norm(keyval[:, 0:kv_width], kv_width).astype(BF16)
+        values = keyval[:, kv_width:].astype(BF16)
+        sendkv[c, every, 0:kv_width] = keys
+        sendkv[c, every, kv_width : 2 * kv_width] = values
+        kv_copy(c).start()
         query = head_norm(dot32(tokens, wq[...]), width)
-        qs[every, :] = query.astype(BF16).astype(F32)
-        keyval = dot32(tokens, wkv[...])
-        keys = head_norm(keyval[:, 0:kv_width], kv_width)
-        duplicate(keys.astype(BF16).astype(F32), kx)
-        duplicate(keyval[:, kv_width:].astype(BF16).astype(F32), vx)
-        top[every, :] = jnp.full((rows_all, 128), -3e38, F32)
-        first_seen = first_ref[0]
-        for t in range(nf):
-            rows = slice(t * slab, rows_all)
-            count = nf - t
+        qs[slot, every, :] = query.astype(BF16).astype(F32)
+        duplicate(keys.astype(F32), kx, slot, 0)
+        duplicate(values.astype(F32), vx, slot, 0)
+
+    def score_half(c, half_id):
+        slab = 2 * pieces[chunks[c][1]][1] // nx
+        slot = c % 2
+        for j in range(nx):
+            rows = slice(j * slab, nx * slab)
+            count = nx - j
             product = (
-                qs[rows, :].reshape(count, slab, width) * per_query_head(kx, t, slab)[None]
+                qs[slot, rows, :].reshape(count, slab, width)
+                * per_query_head(kx, slot, half_id, j, slab)[None]
             ).reshape(count * slab, width)
             high, low = split_two(product)
             score = (dot32(high, pool) + dot32(low, pool)) * score_row
+            frame = 2 * j + (side if half_id == 0 else 1 - side)
+            seen = frame >= first_seen
+            same = score[0:slab]
+            if half_id == 1:
+                same = jnp.where(jnp.logical_and(seen, side == 1), same, -1e30)
             if count > 1:
-                later = jnp.where(t >= first_seen, score[slab:], -1e30)
-                score = jnp.concatenate([score[0:slab], later], axis=0)
-            scores[t, rows, :] = score
+                later = jnp.where(seen, score[slab:], -1e30)
+                score = jnp.concatenate([same, later], axis=0)
+            else:
+                score = same
+            scores[half_id * nx + j, rows, :] = score
             top[rows, :] = jnp.maximum(top[rows, :], score)
+
+    def attend(c):
+        p, piece = chunks[c]
+        rows_all = 2 * pieces[piece][1]
+        slab = rows_all // nx
+        every = slice(0, rows_all)
+        slot = c % 2
+        top[every, :] = jnp.full((rows_all, 128), -3e38, F32)
+        score_half(c, 0)
+        kv_copy(c).wait_recv()
+        keyval = recvkv[c, every, :].astype(F32)
+        duplicate(keyval[:, 0:kv_width], kx, slot, 1)
+        duplicate(keyval[:, kv_width:], vx, slot, 1)
+        score_half(c, 1)
         total[every, :] = jnp.zeros((rows_all, 128), F32)
-        for t in range(nf):
-            rows = slice(t * slab, rows_all)
+        for t in range(2 * nx):
+            rows = slice(t % nx * slab, rows_all)
             weight = jnp.exp(scores[t, rows, :] - top[rows, :])
             scores[t, rows, :] = weight
             total[rows, :] += weight
         attended[every, :] = jnp.zeros((rows_all, width), F32)
-        for t in range(nf):
-            rows = slice(t * slab, rows_all)
-            count = nf - t
+        for t in range(2 * nx):
+            j = t % nx
+            rows = slice(j * slab, rows_all)
+            count = nx - j
             probs = (scores[t, rows, :] / total[rows, :]).astype(BF16)
             spread_probs = dot32(probs, spread_heads)
             attended[rows, :] += (
-                spread_probs.reshape(count, slab, width) * per_query_head(vx, t, slab)[None]
+                spread_probs.reshape(count, slab, width)
+                * per_query_head(vx, slot, t // nx, j, slab)[None]
             ).reshape(count * slab, width)
+        tokens = recvh[piece][p].reshape(rows_all, width)
         output = dot32(attended[every, :].astype(BF16), wo[...])
-        sendo[piece][p] = (tokens.astype(F32) + output).astype(BF16).reshape(nf, slab, width)
+        sendo[piece][p] = (tokens.astype(F32) + output).astype(BF16).reshape(nx, slab, width)
         f_start(*home_args(c))
 
     pending = list(range(early, steps))
@@ -505,27 +562,33 @@
     last = len(chunks)
     exchange(0)
     next_sum()
-    for c in range(1, last):
-        exchange(c)
-        if c == 1:
-            next_sum()
-        attend(c - 1)
-    attend(last - 1)
+    project(0)
+    exchange(1)
+    next_sum()
+    project(1)
+    attend(0)
+    exchange(2)
+    attend(1)
+    project(2)
+    exchange(3)
+    project(3)
+    attend(2)
+    attend(3)
     while pending:
         next_sum()
 
     for c in range(last):
         p, piece = chunks[c]
         start, span = pieces[piece]
-        slab = 2 * span // nf
+        slab = 2 * span // nx
         f_wait(*home_args(c))
         for r in range(2):
-            for k in range(nf // 2):
+            for k in range(nx // 2):
                 first = start + k * slab
                 used = min(slab, local - first)
                 if used > 0:
                     out_ref[2 * p + r, first : first + used, :] = recvo[piece][
-                        p, r * nf // 2 + k, 0:used, :
+                        p, r * nx // 2 + k, 0:used, :
                     ]
 
     for p in range(2):
@@ -534,6 +597,7 @@
         z_sent(*back_args(c))
         f_sent(*out_args(c))
         f_sent(*home_args(c))
+        kv_copy(c).wait_send()
 
 
 def body(
@@ -563,8 +627,9 @@
     kv_heads = w_keyval.shape[1] // 2 // hd
     padded = -(-local // 16) * 16
     wide = -(-modes // 128) * 128
-    units = 2 * padded // nf // 8
-    split = (units + 1) // 2 * 4 * nf
+    nx = nf // 2
+    units = 2 * padded // nx // 16
+    split = (units + 1) // 2 * 8 * nx
     pieces = ((0, split), (split, padded - split))
     rows_all = 2 * split
     geo = dict(
@@ -606,12 +671,14 @@
             pltpu.VMEM((128, 128), F32),
         ]
         + [pltpu.VMEM((2, n, padded, 128), BF16)] * 4
-        + [pltpu.VMEM((2, nf, 2 * pieces[0][1] // nf, width), BF16)] * 4
-        + [pltpu.VMEM((2, nf, 2 * pieces[1][1] // nf, width), BF16)] * 4
+        + [pltpu.VMEM((2, nx, 2 * pieces[0][1] // nx, width), BF16)] * 4
+        + [pltpu.VMEM((2, nx, 2 * pieces[1][1] // nx, width), BF16)] * 4
         + [
-            pltpu.VMEM((rows_all, width), F32),
-            pltpu.VMEM((rows_all, kv_heads * 128), F32),
-            pltpu.VMEM((rows_all, kv_heads * 128), F32),
+            pltpu.VMEM((4, rows_all, w_keyval.shape[1]), BF16),
+            pltpu.VMEM((4, rows_all, w_keyval.shape[1]), BF16),
+            pltpu.VMEM((2, rows_all, width), F32),
+            pltpu.VMEM((2, 2, rows_all, kv_heads * 128), F32),
+            pltpu.VMEM((2, 2, rows_all, kv_heads * 128), F32),
             pltpu.VMEM((nf, rows_all, 128), F32),
             pltpu.VMEM((rows_all, 128), F32),
             pltpu.VMEM((rows_all, 128), F32),
@@ -623,6 +690,8 @@
             pltpu.SemaphoreType.DMA((3,)),
             pltpu.SemaphoreType.DMA((6,)),
             pltpu.SemaphoreType.DMA((8,)),
+            pltpu.SemaphoreType.DMA((4,)),
+            pltpu.SemaphoreType.DMA((4,)),
             pltpu.SemaphoreType.DMA((6, n - 1)),
             pltpu.SemaphoreType.DMA((6, n - 1)),
             pltpu.SemaphoreType.DMA((8, nf)),

time: 148 us -> 133 us (0.90)
  the two profiles are of different devices: /device:TPU:136 before, /device:TPU:1 now
where the time goes in v3:
time: 133 us; the launch traced here: 131 us
  Pallas kernels  122 us (92%)
  local copies, waits for them, and re-layouts  7.52 us (6%)
    pallas_call x1, Pallas kernels, body(): pl.pallas_call(functools.partial(layer_kernel, geo), out_shape=(jax.Shape...  122 us
    unnamed x4, local copies, waits for them, and re-layouts  7.52 us

profile of v3, /device:TPU:1, one launch (start us, length us, event | category | flops | bytes accessed | tf_op | source)
XLA Modules:
  0.0 130.8 jit_solution(8175087313520862869)
XLA Ops:
  1.3 2.2 %copy.23 = bf16[1,1,4,90,1024]{4,3,2,1,0:T(8,128)(2,1)} copy(bf16[1,1,4,90,1024]{4,2,3,1,0:T(4,128)(2,1)} %param.16) | data formatting | bytes 1474560 | tf_op args[0]
  3.5 122.0 %layer.1 = (bf16[4,90,1024]{2,1,0:T(8,128)(2,1)}, f32[128,64]{1,0:T(8,128)}, f32[2,64]{1,0:T(2,128)}) custom-call(s32[1]{0:T(128)S(6)} %copy.26.first_ref, s32[1,4]{1,0:T(1,128)} %band_ref.1, f32[16]{0:T(128)} %heads_ref.1, bf16[4,90,1024]{2,1,0:T(8,128)(2,1)} %bitcast.13, bf16[720,1024]{1,0:T(8,128)(2,1)} %lat_ref.1, f32[1,1024]{1,0:T(1,128)} %bitcast.19, ...), custom_call_target="tpu_custom_call" | custom-call | tf_op jit(solution)/shard_map/layer/pallas_call | solution.py:654
  125.5 2.6 %copy.20 = bf16[1,1,4,90,1024]{4,2,3,1,0:T(4,128)(2,1)} copy(bf16[1,1,4,90,1024]{4,3,2,1,0:T(8,128)(2,1)} %bitcast.14) | data formatting | bytes 1474560
  128.1 1.5 %copy.27 = f32[2,1,64,64]{3,2,1,0:T(8,128)} copy(f32[2,1,64,64]{3,2,1,0:T(8,128)} %bitcast.16) | data formatting | bytes 65536
  129.6 1.2 copy.28

commit v4 on v3

--- a/solution.py
+++ b/solution.py
@@ -64,6 +64,7 @@
     grad_ref,
     bias_ref,
     embed,
+    inputs_ref,
     wq,
     wkv,
     wo,
@@ -292,7 +293,8 @@
     half = lanes_below((local, 128), 64)
 
     def normalize(p, r):
-        cells = fields_ref[2 * p + r].astype(F32) + embed[2 * p + r]
+        cells = fields_ref[:, 2 * p + r, :].astype(F32) + embed[2 * p + r]
+        inputs_ref[2 * p + r] = cells
         cells = cells - jnp.mean(cells, axis=-1, keepdims=True)
         spread = jnp.mean(cells * cells, axis=-1, keepdims=True)
         return cells * lax.rsqrt(spread + 1e-05) * gain_ref[...]
@@ -462,8 +464,7 @@
                 jnp.where(near_half, pltpu.roll(even, 64, 1), odd),
             )
             for r in range(2):
-                inputs = fields_ref[2 * p + r, start : start + count, lanes].astype(F32)
-                inputs = inputs + embed[2 * p + r, :, lanes]
+                inputs = inputs_ref[2 * p + r, start : start + count, lanes]
                 hidden = (inputs + grid_rows[r]).astype(BF16)
                 for k in range(nx // 2):
                     used = min(slab, count - k * slab)
@@ -559,6 +560,20 @@
         if pending:
             finish_sum(pending.pop(0))
 
+    def deliver(c):
+        p, piece = chunks[c]
+        start, span = pieces[piece]
+        slab = 2 * span // nx
+        f_wait(*home_args(c))
+        for r in range(2):
+            for k in range(nx // 2):
+                first = start + k * slab
+                used = min(slab, local - first)
+                if used > 0:
+                    out_ref[2 * p + r, first : first + used, :] = recvo[piece][
+                        p, r * nx // 2 + k, 0:used, :
+                    ]
+
     last = len(chunks)
     exchange(0)
     next_sum()
@@ -571,25 +586,16 @@
     attend(1)
     project(2)
     exchange(3)
+    deliver(0)
+    deliver(1)
     project(3)
     attend(2)
     attend(3)
     while pending:
         next_sum()
 
-    for c in range(last):
-        p, piece = chunks[c]
-        start, span = pieces[piece]
-        slab = 2 * span // nx
-        f_wait(*home_args(c))
-        for r in range(2):
-            for k in range(nx // 2):
-                first = start + k * slab
-                used = min(slab, local - first)
-                if used > 0:
-                    out_ref[2 * p + r, first : first + used, :] = recvo[piece][
-                        p, r * nx // 2 + k, 0:used, :
-                    ]
+    deliver(2)
+    deliver(3)
 
     for p in range(2):
         z_sent(send1, recv1, p, p, whole)
@@ -598,6 +604,11 @@
         f_sent(*out_args(c))
         f_sent(*home_args(c))
         kv_copy(c).wait_send()
+
+
+def keep(grads_ref, bias_ref, grads_out, bias_out):
+    grads_out[...] = grads_ref[...]
+    bias_out[...] = bias_ref[...]
 
 
 def body(
@@ -662,6 +673,7 @@
         out_specs=(vmem, vmem, vmem),
         scratch_shapes=[
             pltpu.VMEM((lat_rows, 1, width), F32),
+            pltpu.VMEM((lat_rows, local, width), F32),
             pltpu.VMEM(w_query.shape, BF16),
             pltpu.VMEM(w_keyval.shape, BF16),
             pltpu.VMEM(w_output.shape, BF16),
@@ -707,7 +719,7 @@
         earliest_past_snapshot,
         band_rows,
         score_scale,
-        fields.reshape(lat_rows, local, width),
+        fields.reshape(lat_rows, local, width).transpose(1, 0, 2),
         lat_table,
         norm_gain.reshape(1, width),
         w_in1.reshape(2, block, block),
@@ -721,6 +733,16 @@
         w_keyval,
         w_output,
     )
+    grads, bias = pl.pallas_call(
+        keep,
+        out_shape=(
+            jax.ShapeDtypeStruct(grads.shape, F32),
+            jax.ShapeDtypeStruct(bias.shape, F32),
+        ),
+        in_specs=[vmem] * 2,
+        out_specs=(vmem, vmem),
+        name="sums",
+    )(grads, bias)
     return (
         out.reshape(fields.shape),
         grads.reshape(2, 1, block, block),

time: 133 us -> 129 us (0.970)
  local copies, waits for them, and re-layouts: 7.52 us -> 2.57 us
    unnamed x4 -> x1, local copies, waits for them, and re-layouts: 7.52 us -> 2.57 us
    pallas_call x0 -> x1, Pallas kernels: none -> 1.48 us  [body(): pl.pallas_call(keep, out_shape=(jax.ShapeDtypeStruct(grads.shape, F32), j...]
where the time goes in v4:
time: 129 us; the launch traced here: 127 us
  Pallas kernels  123 us (95%)
  local copies, waits for them, and re-layouts  2.57 us (2%)
  between operations  1.29 us (1%)
    pallas_call x1, Pallas kernels, body(): pl.pallas_call(functools.partial(layer_kernel, geo), out_shape=(jax.Shape...  122 us

profile of v4, /device:TPU:1, one launch (start us, length us, event | category | flops | bytes accessed | tf_op | source)
XLA Modules:
  0.0 127.3 jit_solution(17964323983197392935)
XLA Ops:
  1.3 122.0 %layer.1 = (bf16[4,90,1024]{2,1,0:T(8,128)(2,1)}, f32[128,64]{1,0:T(8,128)}, f32[2,64]{1,0:T(2,128)}) custom-call(s32[1]{0:T(128)S(6)} %copy.21.first_ref, s32[1,4]{1,0:T(1,128)} %band_ref.1, f32[16]{0:T(128)} %heads_ref.1, bf16[90,4,1024]{2,1,0:T(4,128)(2,1)} %bitcast.14, bf16[720,1024]{1,0:T(8,128)(2,1)} %lat_ref.1, f32[1,1024]{1,0:T(1,128)} %bitcast.18, ...), custom_call_target="tpu_custom_call" | custom-call | tf_op jit(solution)/shard_map/layer/pallas_call | solution.py:665
  123.3 2.6 %copy.19 = bf16[1,1,4,90,1024]{4,2,3,1,0:T(4,128)(2,1)} copy(bf16[1,1,4,90,1024]{4,3,2,1,0:T(8,128)(2,1)} %bitcast.13) | data formatting | bytes 1474560
  125.9 1.5 %sums.1 = (f32[128,64]{1,0:T(8,128)}, f32[2,64]{1,0:T(2,128)}) custom-call(f32[128,64]{1,0:T(8,128)} %get-tuple-element.9.grads_ref, f32[2,64]{1,0:T(2,128)} %get-tuple-element.10.bias_ref), custom_call_target="tpu_custom_call" | custom-call | tf_op jit(solution)/shard_map/sums/pallas_call | solution.py:736

commit v5 on v4

--- a/solution.py
+++ b/solution.py
@@ -570,7 +570,7 @@
                 first = start + k * slab
                 used = min(slab, local - first)
                 if used > 0:
-                    out_ref[2 * p + r, first : first + used, :] = recvo[piece][
+                    out_ref[first : first + used, 2 * p + r, :] = recvo[piece][
                         p, r * nx // 2 + k, 0:used, :
                     ]
 
@@ -665,7 +665,7 @@
     out, grads, bias = pl.pallas_call(
         functools.partial(layer_kernel, geo),
         out_shape=(
-            jax.ShapeDtypeStruct((lat_rows, local, width), BF16),
+            jax.ShapeDtypeStruct((local, lat_rows, width), BF16),
             jax.ShapeDtypeStruct((2 * block, block), F32),
             jax.ShapeDtypeStruct((2, block), F32),
         ),
@@ -744,7 +744,7 @@
         name="sums",
     )(grads, bias)
     return (
-        out.reshape(fields.shape),
+        out.transpose(1, 0, 2).reshape(fields.shape),
         grads.reshape(2, 1, block, block),
         bias,
     )

time: 129 us -> 129 us (level)
  no operation moved by 1% of the time
where the time goes in v5:
time: 129 us; the launch traced here: 127 us
  Pallas kernels  123 us (95%)
  local copies, waits for them, and re-layouts  2.23 us (2%)
  between operations  1.29 us (1%)
    pallas_call x1, Pallas kernels, body(): pl.pallas_call(functools.partial(layer_kernel, geo), out_shape=(jax.Shape...  122 us

profile of v5, /device:TPU:1, one launch (start us, length us, event | category | flops | bytes accessed | tf_op | source)
XLA Modules:
  0.0 127.0 jit_solution(11355423203950427544)
XLA Ops:
  1.3 122.0 %layer.1 = (bf16[90,4,1024]{2,1,0:T(4,128)(2,1)}, f32[128,64]{1,0:T(8,128)}, f32[2,64]{1,0:T(2,128)}) custom-call(s32[1]{0:T(128)S(6)} %copy.21.first_ref, s32[1,4]{1,0:T(1,128)} %band_ref.1, f32[16]{0:T(128)} %heads_ref.1, bf16[90,4,1024]{2,1,0:T(4,128)(2,1)} %bitcast.15, bf16[720,1024]{1,0:T(8,128)(2,1)} %lat_ref.1, f32[1,1024]{1,0:T(1,128)} %bitcast.20, ...), custom_call_target="tpu_custom_call" | custom-call | tf_op jit(solution)/shard_map/layer/pallas_call | solution.py:665
  123.3 1.5 %sums.1 = (f32[128,64]{1,0:T(8,128)}, f32[2,64]{1,0:T(2,128)}) custom-call(f32[128,64]{1,0:T(8,128)} %get-tuple-element.9.grads_ref, f32[2,64]{1,0:T(2,128)} %get-tuple-element.10.bias_ref), custom_call_target="tpu_custom_call" | custom-call | tf_op jit(solution)/shard_map/sums/pallas_call | solution.py:736
  124.8 2.2 %copy.22 = bf16[1,1,4,90,1024]{4,2,3,1,0:T(4,128)(2,1)} copy(bf16[1,1,4,90,1024]{4,2,3,1,0:T(4,128)(2,1)} %bitcast.16) | data formatting | bytes 1474560
